TPU v7x, 256 devices: a whole 4x4x8 slice. The times are simulated.
256 devices in a mesh: dp: 8 (over x, core), code: 32 (over z, y).
Axes of the slice: x: 4, y: 4, z: 8, core: 2. Of those that a mesh axis runs over, the one named last changes fastest.
Arguments:
- latents: bfloat16 [4096, 256], P(('dp', 'code')), may hold values from -1000 to 1000
- out_grad: bfloat16 [4096, 256], P(('dp', 'code')), may hold values from -6 to 6
- targets: int32 [4096], P('dp'), may hold values from 0 to 262143
- codebook: bfloat16 [262144, 256], P('code'), may hold values from -2 to 2
Outputs:
- latent_grad: bfloat16 [4096, 256], P(('dp', 'code'))
- codebook_grad: float32 [262144, 256], P(('code', 'dp'))
- token_loss: float32 [4096], P(('dp', 'code'))
All inputs are finite; a program needn't handle non-finite values.
Results may differ from a plain program's by a relative error of at most 0.0042.
Values may be sent and summed in bfloat16 or wider, within the bound.
No kernel may reach another device: no remote copies, remote signals or barrier semaphores. Data moves between devices by JAX's collectives and lax.ppermute only.
A program may use at most 128 MiB of HBM per device.

v0:
```python
import functools

import jax
import jax.numpy as jnp
from jax import lax
from jax.experimental import pallas as pl
from jax.experimental.pallas import tpu as pltpu
from jax.sharding import Mesh
from jax.sharding import PartitionSpec as P

ce_weight = 1.0
F32 = jnp.float32
BF16 = jnp.bfloat16
NT = (((1,), (1,)), ((), ()))
NN = (((1,), (0,)), ((), ()))
ZY = ("z", "y")
XC = ("x", "core")
VMEM_LIMIT = 32 << 20


def dot(a, b, dims, precision=None):
    return lax.dot_general(a, b, dims, preferred_element_type=F32, precision=precision)


def params(**kw):
    return pltpu.CompilerParams(vmem_limit_bytes=VMEM_LIMIT, **kw)


def cost(flops, bytes_accessed, trans=0):
    return pl.CostEstimate(flops=flops, bytes_accessed=bytes_accessed, transcendentals=trans)


def pick_kernel(cb, tgt_ref, book_ref, out_ref):
    i = pl.program_id(0)

    @pl.when(i == 0)
    def _():
        out_ref[...] = jnp.zeros_like(out_ref)

    tokens = tgt_ref.shape[0]
    ids = lax.broadcasted_iota(jnp.int32, (tokens, cb), 1) + i * cb
    hit = jnp.where(ids == tgt_ref[:, :1], 1.0, 0.0).astype(BF16)
    out_ref[...] += dot(hit, book_ref[...], NN)


def pick_rows(tgt_cols, book):
    tokens, codes, d = tgt_cols.shape[0], *book.shape
    cb = 1024
    return pl.pallas_call(
        functools.partial(pick_kernel, cb),
        grid=(codes // cb,),
        in_specs=[
            pl.BlockSpec((tokens, 128), lambda i: (0, 0)),
            pl.BlockSpec((cb, d), lambda i: (i, 0)),
        ],
        out_specs=pl.BlockSpec((tokens, d), lambda i: (0, 0)),
        out_shape=pltpu.HBM((tokens, d), F32),
        compiler_params=params(),
        cost_estimate=cost(2 * tokens * codes * d, codes * d * 2),
        name="pick",
    )(tgt_cols, book)


def stats_kernel(steps, lat_ref, grad_ref, rows_ref, book_ref, out_ref, m_col, mean_col, m_s, l_s, w_s):
    i = pl.program_id(0)

    @pl.when(i == 0)
    def _():
        m_s[...] = jnp.full_like(m_s, -jnp.inf)
        l_s[...] = jnp.zeros_like(l_s)
        w_s[...] = jnp.zeros_like(w_s)

    block = book_ref[...]
    cb, tokens = block.shape[0], lat_ref.shape[0]
    logit = dot(block, lat_ref[...], NT).reshape(cb // 8, 8, tokens)
    back = dot(block, grad_ref[...], NT).reshape(cb // 8, 8, tokens)
    old = m_s[...]
    new = jnp.maximum(old, jnp.max(logit, axis=0))
    factor = jnp.exp(old - new)
    expo = jnp.exp(logit - new[None])
    l_s[...] = l_s[...] * factor + jnp.sum(expo, axis=0)
    w_s[...] = w_s[...] * factor + jnp.sum(expo * back, axis=0)
    m_s[...] = new

    @pl.when(i == steps - 1)
    def _():
        m = m_s[...]
        top = jnp.max(m, axis=0, keepdims=True)
        scale = jnp.exp(m - top)
        total = jnp.sum(l_s[...] * scale, axis=0, keepdims=True)
        weighted = jnp.sum(w_s[...] * scale, axis=0, keepdims=True)
        prod = lat_ref[...].astype(F32) * rows_ref[...]
        picked = dot(jnp.ones((8, prod.shape[1]), F32), prod, NT, lax.Precision.HIGHEST)[:1]
        pack = jnp.concatenate([top, total, weighted, picked], axis=0)
        out_ref[...] = jnp.broadcast_to(pack[None], out_ref.shape)
        m_col[...] = jnp.broadcast_to(top, (128, tokens)).T
        mean_col[...] = jnp.broadcast_to(weighted / total, (128, tokens)).T


def local_stats(toks, rows, book, peers):
    tokens, (codes, d) = toks.shape[0], book.shape
    cb = 1024
    steps = codes // cb
    return pl.pallas_call(
        functools.partial(stats_kernel, steps),
        grid=(steps,),
        in_specs=[
            pl.BlockSpec((tokens, d), lambda i: (0, 0)),
            pl.BlockSpec((tokens, d), lambda i: (0, 1)),
            pl.BlockSpec((tokens, d), lambda i: (0, 0)),
            pl.BlockSpec((cb, d), lambda i: (i, 0)),
        ],
        out_specs=[
            pl.BlockSpec((peers, 4, tokens), lambda i: (0, 0, 0)),
            pl.BlockSpec((tokens, 128), lambda i: (0, 0)),
            pl.BlockSpec((tokens, 128), lambda i: (0, 0)),
        ],
        out_shape=[
            jax.ShapeDtypeStruct((peers, 4, tokens), F32),
            pltpu.HBM((tokens, 128), F32),
            pltpu.HBM((tokens, 128), F32),
        ],
        scratch_shapes=[pltpu.VMEM((8, tokens), F32)] * 3,
        compiler_params=params(),
        cost_estimate=cost(4 * tokens * codes * d, codes * d * 2, tokens * codes),
        name="stats",
    )(toks, toks, rows, book)


def lat_step(lat_ref, grad_ref, m_ref, mean_ref, book_ref, a_ref, b_ref):
    block = book_ref[...]
    logit = dot(lat_ref[...], block, NT)
    back = dot(grad_ref[...], block, NT)
    expo = jnp.exp(logit - m_ref[:, :1])
    dev = expo * (back - mean_ref[:, :1])
    a_ref[...] += dot(dev.astype(BF16), block, NN)
    b_ref[...] += dot(expo.astype(BF16), block, NN)


def first_kernel(lat_ref, grad_ref, m_ref, mean_ref, book_ref, a_ref, b_ref):
    @pl.when(pl.program_id(0) == 0)
    def _():
        a_ref[...] = jnp.zeros_like(a_ref)
        b_ref[...] = jnp.zeros_like(b_ref)

    lat_step(lat_ref, grad_ref, m_ref, mean_ref, book_ref, a_ref, b_ref)


def second_kernel(
    steps, lat_ref, grad_ref, m_ref, mean_ref, book_ref, a0, b0, rows_ref, all_ref, part_ref, a_ref, b_ref
):
    @pl.when(pl.program_id(0) == 0)
    def _():
        a_ref[...] = a0[...]
        b_ref[...] = b0[...]

    lat_step(lat_ref, grad_ref, m_ref, mean_ref, book_ref, a_ref, b_ref)

    @pl.when(pl.program_id(0) == steps - 1)
    def _():
        tokens = m_ref.shape[0]
        lse = jnp.broadcast_to(all_ref[0, 0:1, :], (128, tokens)).T
        mean = jnp.broadcast_to(all_ref[0, 1:2, :], (128, tokens)).T
        own = jnp.exp(m_ref[...] - lse)
        ratio = own * (ce_weight + mean_ref[...] - mean)
        part = own[:, :1] * a_ref[...] + ratio[:, :1] * b_ref[...] - ce_weight * rows_ref[...]
        part_ref[...] = part.astype(part_ref.dtype)


def lat_specs(tokens, d, cb, first):
    return [
        pl.BlockSpec((tokens, d), lambda i: (0, 0)),
        pl.BlockSpec((tokens, d), lambda i: (0, 1)),
        pl.BlockSpec((tokens, 128), lambda i: (0, 0)),
        pl.BlockSpec((tokens, 128), lambda i: (0, 0)),
        pl.BlockSpec((cb, d), lambda i: (i + first, 0)),
    ]


def lat_first(toks, m_col, mean_col, book):
    tokens, (codes, d) = toks.shape[0], book.shape
    cb = 1024
    whole = pl.BlockSpec((tokens, d), lambda i: (0, 0))
    return pl.pallas_call(
        first_kernel,
        grid=(codes // cb // 2,),
        in_specs=lat_specs(tokens, d, cb, 0),
        out_specs=[whole] * 2,
        out_shape=[pltpu.HBM((tokens, d), F32)] * 2,
        compiler_params=params(),
        cost_estimate=cost(4 * tokens * codes * d, codes * d, tokens * codes // 2),
        name="lat_first",
    )(toks, toks, m_col, mean_col, book)


def lat_second(toks, m_col, mean_col, book, a, b, rows, row):
    tokens, (codes, d) = toks.shape[0], book.shape
    cb = 1024
    steps = codes // cb // 2
    whole = pl.BlockSpec((tokens, d), lambda i: (0, 0))
    return pl.pallas_call(
        functools.partial(second_kernel, steps),
        grid=(steps,),
        in_specs=lat_specs(tokens, d, cb, steps)
        + [whole] * 3
        + [pl.BlockSpec((1, 4, tokens), lambda i: (0, 0, 0))],
        out_specs=whole,
        out_shape=jax.ShapeDtypeStruct((tokens, d), BF16),
        scratch_shapes=[pltpu.VMEM((tokens, d), F32)] * 2,
        compiler_params=params(),
        cost_estimate=cost(4 * tokens * codes * d, codes * d, tokens * codes // 2),
        name="lat_second",
    )(toks, toks, m_col, mean_col, book, a, b, rows, row)


def combine_kernel(all_ref, tgt_ref, row_ref, loss_ref):
    stats = all_ref[...]
    m, l, w = stats[:, 0, :], stats[:, 1, :], stats[:, 2, :]
    top = jnp.max(m, axis=0, keepdims=True)
    scale = jnp.exp(m - top)
    total = jnp.sum(l * scale, axis=0, keepdims=True)
    mean = jnp.sum(w * scale, axis=0, keepdims=True) / total
    lse = top + jnp.log(total)
    pack = jnp.concatenate([lse, mean, tgt_ref[...].astype(F32), mean], axis=0)
    row_ref[...] = jnp.broadcast_to(pack[None], row_ref.shape)
    loss_ref[...] = lse - jnp.sum(stats[:, 3, :], axis=0, keepdims=True)


def combine(stats, tgt, groups):
    tokens = stats.shape[-1]
    return pl.pallas_call(
        combine_kernel,
        out_shape=[
            jax.ShapeDtypeStruct((groups, 4, tokens), F32),
            jax.ShapeDtypeStruct((1, tokens), F32),
        ],
        compiler_params=params(),
        cost_estimate=cost(tokens * 1000, tokens * 800),
        name="combine",
    )(stats, tgt)


def book_kernel(groups, s_ref, rows_ref, book_ref, *rest):
    toks, (out_ref, buf, sem) = rest[:groups], rest[groups:]
    for g in range(groups):
        pltpu.make_async_copy(toks[g], buf.at[g], sem.at[g]).start()
    block = book_ref[...]
    cb, d = block.shape
    out_ref[...] = jnp.zeros_like(out_ref)

    def step(g, carry):
        pltpu.make_async_copy(toks[0], buf.at[g], sem.at[g]).wait()
        row = rows_ref[s_ref[g]]
        tokens = row.shape[1]
        both = buf[g]
        lat, grad = both[:, :d], both[:, d:]
        logit = dot(block, lat, NT)
        back = dot(block, grad, NT)
        prob = jnp.exp(logit - row[0:1])
        ids = lax.broadcasted_iota(jnp.int32, (cb, tokens), 0)
        hit = jnp.where(ids == row[2:3].astype(jnp.int32) - s_ref[groups], 1.0, 0.0)
        delta = prob * (back - row[1:2]) + ce_weight * (prob - hit)
        out_ref[...] += dot(delta.astype(BF16), lat, NN) + dot(hit.astype(BF16), grad, NN)
        return carry

    lax.fori_loop(0, groups, step, 0)


def book_grad(scalars, rows, book, toks):
    groups = len(toks)
    (tokens, width), (chunk, d) = toks[0].shape, book.shape
    grid_spec = pltpu.PrefetchScalarGridSpec(
        num_scalar_prefetch=1,
        grid=(1,),
        in_specs=[
            pl.BlockSpec((groups, 4, tokens), lambda i, s: (0, 0, 0)),
            pl.BlockSpec((chunk, d), lambda i, s: (0, 0)),
        ]
        + [pl.BlockSpec(memory_space=pl.ANY)] * groups,
        out_specs=pl.BlockSpec((chunk, d), lambda i, s: (0, 0)),
        scratch_shapes=[
            pltpu.VMEM((groups, tokens, width), BF16),
            pltpu.SemaphoreType.DMA((groups,)),
        ],
    )
    return pl.pallas_call(
        functools.partial(book_kernel, groups),
        grid_spec=grid_spec,
        out_shape=jax.ShapeDtypeStruct((chunk, d), F32),
        compiler_params=params(),
        cost_estimate=cost(
            8 * groups * tokens * chunk * d, groups * tokens * width * 2, groups * tokens * chunk
        ),
        name="book_grad",
    )(scalars, rows, book, *toks)


def in_hbm(*arrays):
    return [pltpu.with_memory_space_constraint(x, pltpu.HBM) for x in arrays]


def per_device(latents, out_grad, targets, codebook):
    peers = lax.axis_size("z") * lax.axis_size("y")
    nx = lax.axis_size("x")
    own_count, d = latents.shape
    code_dev = codebook.shape[0]
    tokens = own_count * peers
    code_pos = lax.axis_index(ZY)
    x_pos, core = lax.axis_index("x"), lax.axis_index("core")
    dp_pos, chunk = x_pos * 2 + core, code_dev // (2 * nx)
    swap = [(0, 1), (1, 0)]
    book = pltpu.with_memory_space_constraint(codebook, pltpu.HBM)

    both = jnp.concatenate([latents, out_grad], axis=1)
    toks = lax.all_to_all(jnp.broadcast_to(both[None], (peers, own_count, 2 * d)), ZY, 0, 0)
    toks = toks.reshape(tokens, 2 * d)
    local_ids = targets - code_pos * code_dev
    rows = pick_rows(jnp.broadcast_to(local_ids[:, None], (tokens, 128)), book)
    (rows,) = in_hbm(rows)
    places = [lax.rem(x_pos + nx - k, nx) * 2 for k in range(nx)]
    scalars = [p + core for p in places] + [p + 1 - core for p in places]
    scalars += [code_pos * code_dev + dp_pos * chunk]
    scalars = jnp.stack(scalars).astype(jnp.int32)
    own_book = lax.dynamic_slice(codebook, (dp_pos * chunk, 0), (chunk, d))
    packed, m_col, mean_col = local_stats(toks, rows, book, peers)
    m_col, mean_col = in_hbm(m_col, mean_col)
    stats = lax.all_to_all(packed, ZY, 0, 0)
    late = lax.optimization_barrier((toks, packed))[0]
    same = [late]
    for k in range(1, nx):
        same.append(lax.ppermute(late, "x", [(i, (i + k) % nx) for i in range(nx)]))
    a, b = lat_first(toks, m_col, mean_col, book)
    row, loss = combine(stats, targets[None], 2 * nx)
    everyone = lax.all_to_all(row, XC, 0, 0)
    part = lat_second(toks, m_col, mean_col, book, *in_hbm(a, b), rows, row)
    part, everyone = lax.optimization_barrier((part, everyone))
    moved = lax.all_to_all(part.reshape(peers, own_count, d), ZY, 0, 0)
    latent_grad = jnp.sum(moved.astype(F32), axis=0).astype(BF16)
    token_loss = lax.dynamic_slice(loss, (0, code_pos * own_count), (1, own_count)).reshape(own_count)

    other = []
    for piece in same:
        other.append(lax.ppermute(piece, "core", swap))
    codebook_grad = book_grad(scalars, everyone, own_book, same + other)
    return latent_grad, codebook_grad, token_loss


def solution(mesh):
    shape = (mesh.shape["dp"] // 2, 2, mesh.shape["code"] // 4, 4)
    fine = Mesh(mesh.devices.reshape(shape), ("x", "core", "z", "y"))
    dp, code = ("x", "core"), ("z", "y")
    in_specs = (P(dp + code, None), P(dp + code, None), P(dp), P(code, None))
    out_specs = (P(dp + code, None), P(code + dp, None), P(dp + code))
    return jax.shard_map(
        per_device, mesh=fine, in_specs=in_specs, out_specs=out_specs, check_vma=False
    )
```

profile of v0, /device:TPU:1, one launch (start us, length us, event | category | flops | bytes accessed | tf_op | source)
XLA Modules:
  0.0 110.5 jit_solution(3898146401710932050)
XLA Ops:
  0.6 0.7 pad_maximum_fusion
  1.3 0.9 broadcast_in_dim.6
  2.2 12.0 %all-to-all-start = ((bf16[32,16,512]{2,1,0:T(8,128)(2,1)}), bf16[32,16,512]{2,1,0:T(8,128)(2,1)S(1)}, u32[]{:S(2)}, u32[]{:S(2)}) async-start(bf16[32,16,512]{2,1,0:T(8,128)(2,1)} %broadcast_in_dim.6), calls=%async_computation | async-start | bytes 1048576 | tf_op jit(solution)/shard_map/all_to_all | solution.py:315
  14.2 0.7 broadcast_subtract_fusion
  15.1 7.7 %pick.1.rows_ref = f32[512,256]{1,0:T(8,128)} custom-call(s32[512,128]{1,0:T(8,128)S(1)} %broadcast_in_dim.7.tgt_ref, bf16[8192,256]{1,0:T(8,128)(2,1)} %book_ref.7), custom_call_target="tpu_custom_call" | custom-call | flops 2147483648 | bytes 4194304 | tf_op jit(solution)/shard_map/pick/pallas_call | solution.py:49
  22.8 7.7 %all-to-all-done = bf16[32,16,512]{2,1,0:T(8,128)(2,1)S(1)} async-done(((bf16[32,16,512]{2,1,0:T(8,128)(2,1)}), bf16[32,16,512]{2,1,0:T(8,128)(2,1)S(1)}, u32[]{:S(2)}, u32[]{:S(2)}) %all-to-all-start) | async-done | bytes 524320 | tf_op jit(solution)/shard_map/all_to_all | solution.py:315
  30.5 10.5 %stats.1 = (f32[32,4,512]{2,1,0:T(4,128)}, f32[512,128]{1,0:T(8,128)}, f32[512,128]{1,0:T(8,128)}) custom-call(bf16[512,512]{1,0:T(8,128)(2,1)S(1)} %bitcast.14, bf16[512,512]{1,0:T(8,128)(2,1)S(1)} %bitcast.15, f32[512,256]{1,0:T(8,128)} %pick.1.rows_ref, bf16[8192,256]{1,0:T(8,128)(2,1)} %book_ref.7), custom_call_target="tpu_custom_call" | custom-call | flops 4294967296 | bytes 4194304 | tf_op jit(solution)/shard_map/stats/pallas_call | solution.py:104
  41.0 1.2 %collective-permute-start = (bf16[512,512]{1,0:T(8,128)(2,1)S(1)}, bf16[512,512]{1,0:T(8,128)(2,1)S(1)}, u32[]{:S(2)}, u32[]{:S(2)}) collective-permute-start(bf16[512,512]{1,0:T(8,128)(2,1)S(1)} %bitcast.16), channel_id=1, source_target_pairs={{0,64},{64,128},{128,192},{192,0},{1,65},{65,129},{129,193},{193,1... | collective-permute-start | bytes 1572872 | tf_op jit(solution)/shard_map/ppermute | solution.py:331
  42.2 2.4 %collective-permute-start.1 = (bf16[512,512]{1,0:T(8,128)(2,1)S(1)}, bf16[512,512]{1,0:T(8,128)(2,1)S(1)}, u32[]{:S(2)}, u32[]{:S(2)}) collective-permute-start(bf16[512,512]{1,0:T(8,128)(2,1)S(1)} %bitcast.17), channel_id=1, source_target_pairs={{0,128},{64,192},{128,0},{192,64},{1,129},{65,193},{129,1},{193,65... | collective-permute-start | bytes 1572872 | tf_op jit(solution)/shard_map/ppermute | solution.py:331
  44.7 1.2 %collective-permute-start.2 = (bf16[512,512]{1,0:T(8,128)(2,1)S(1)}, bf16[512,512]{1,0:T(8,128)(2,1)S(1)}, u32[]{:S(2)}, u32[]{:S(2)}) collective-permute-start(bf16[512,512]{1,0:T(8,128)(2,1)S(1)} %bitcast.18), channel_id=1, source_target_pairs={{0,192},{64,0},{128,64},{192,128},{1,193},{65,1},{129,65},{193,129... | collective-permute-start | bytes 1572872 | tf_op jit(solution)/shard_map/ppermute | solution.py:331
  45.9 5.3 %all-to-all-start.1 = ((f32[32,4,512]{2,1,0:T(4,128)}), f32[32,4,512]{2,1,0:T(4,128)S(1)}, u32[]{:S(2)}, u32[]{:S(2)}) async-start(f32[32,4,512]{2,1,0:T(4,128)} %get-tuple-element.17), calls=%async_computation.1 | async-start | bytes 524288 | tf_op jit(solution)/shard_map/all_to_all | solution.py:327
  51.2 1.1 constant_dynamic-slice_fusion.book_ref
  52.2 2.7 %collective-permute-start.3 = (bf16[512,512]{1,0:T(8,128)(2,1)S(1)}, bf16[512,512]{1,0:T(8,128)(2,1)S(1)}, u32[]{:S(2)}, u32[]{:S(2)}) collective-permute-start(bf16[512,512]{1,0:T(8,128)(2,1)S(1)} %bitcast.19), channel_id=1, source_target_pairs={{0,32},{32,0},{1,33},{33,1},{2,34},{34,2},{3,35},{35,3},{4,36},{36... | collective-permute-start | bytes 1572872 | tf_op jit(solution)/shard_map/ppermute | solution.py:343
  55.0 3.5 %collective-permute-start.4 = (bf16[512,512]{1,0:T(8,128)(2,1)S(1)}, bf16[512,512]{1,0:T(8,128)(2,1)}, u32[]{:S(2)}, u32[]{:S(2)}) collective-permute-start(bf16[512,512]{1,0:T(8,128)(2,1)S(1)} %collective-permute-done.rest_1_), channel_id=1, source_target_pairs={{0,32},{32,0},{1,33},{33,1},{2,34},{34,2},{3,35},{35,3},{4,36},{36... | collective-permute-start | bytes 1572872 | tf_op jit(solution)/shard_map/ppermute | solution.py:343
  58.5 7.0 %collective-permute-done.1.rest_2_ = bf16[512,512]{1,0:T(8,128)(2,1)S(1)} collective-permute-done((bf16[512,512]{1,0:T(8,128)(2,1)S(1)}, bf16[512,512]{1,0:T(8,128)(2,1)S(1)}, u32[]{:S(2)}, u32[]{:S(2)}) %collective-permute-start.1) | collective-permute-done | bytes 524320 | tf_op jit(solution)/shard_map/ppermute | solution.py:331
  65.5 3.3 %collective-permute-start.5 = (bf16[512,512]{1,0:T(8,128)(2,1)S(1)}, bf16[512,512]{1,0:T(8,128)(2,1)}, u32[]{:S(2)}, u32[]{:S(2)}) collective-permute-start(bf16[512,512]{1,0:T(8,128)(2,1)S(1)} %collective-permute-done.1.rest_2_), channel_id=1, source_target_pairs={{0,32},{32,0},{1,33},{33,1},{2,34},{34,2},{3,35},{35,3},{4,36},{36... | collective-permute-start | bytes 1572872 | tf_op jit(solution)/shard_map/ppermute | solution.py:343
  68.8 7.7 %lat_first.1 = (f32[512,256]{1,0:T(8,128)}, f32[512,256]{1,0:T(8,128)}) custom-call(bf16[512,512]{1,0:T(8,128)(2,1)S(1)} %bitcast.20, bf16[512,512]{1,0:T(8,128)(2,1)S(1)} %bitcast.21, f32[512,128]{1,0:T(8,128)} %get-tuple-element.13.m_ref, f32[512,128]{1,0:T(8,128)} %get-tuple-element.14.mean_ref, bf16[8192,256]{1,0:T(8,128)(2,1)} %book_ref.7), custom_call_target="tpu_custom_call" | custom-call | flops 4294967296 | bytes 2097152 | tf_op jit(solution)/shard_map/lat_first/pallas_call | solution.py:184
  76.4 0.7 combine.1
  77.2 4.0 %all-to-all-start.2 = ((f32[8,4,512]{2,1,0:T(4,128)}), f32[8,4,512]{2,1,0:T(4,128)S(1)}, u32[]{:S(2)}, u32[]{:S(2)}) async-start(f32[8,4,512]{2,1,0:T(4,128)} %get-tuple-element.18.all_ref), calls=%async_computation.2 | async-start | bytes 131072 | tf_op jit(solution)/shard_map/all_to_all | solution.py:334
  81.2 8.3 %lat_second.1 = bf16[512,256]{1,0:T(8,128)(2,1)} custom-call(bf16[512,512]{1,0:T(8,128)(2,1)S(1)} %bitcast.22, bf16[512,512]{1,0:T(8,128)(2,1)S(1)} %bitcast.23, f32[512,128]{1,0:T(8,128)} %get-tuple-element.13.m_ref, f32[512,128]{1,0:T(8,128)} %get-tuple-element.14.mean_ref, bf16[8192,256]{1,0:T(8,128)(2,1)} %book_ref.7, f32[512,256]{1,0:T(8,128)} %get-tuple-element.15.a0, ...), custom_call_target="tpu_custom_call" | custom-call | flops 4294967296 | bytes 2097152 | tf_op jit(solution)/shard_map/lat_second/pallas_call | solution.py:201
  89.5 0.6 dynamic-slice_bitcast_fusion
  90.1 5.4 %all-to-all-start.3 = ((bf16[32,16,256]{2,1,0:T(8,128)(2,1)}), bf16[32,16,256]{2,1,0:T(8,128)(2,1)}, u32[]{:S(2)}, u32[]{:S(2)}) async-start(bf16[32,16,256]{2,1,0:T(8,128)(2,1)} %bitcast.2), calls=%async_computation.3 | async-start | bytes 524288 | tf_op jit(solution)/shard_map/all_to_all | solution.py:337
  95.5 13.4 %book_grad.1 = f32[1024,256]{1,0:T(8,128)} custom-call(s32[9]{0:T(128)S(1)} %stack.39.s_ref, f32[8,4,512]{2,1,0:T(4,128)S(1)} %all-to-all-done.2.rows_ref, bf16[1024,256]{1,0:T(8,128)(2,1)S(1)} %constant_dynamic-slice_fusion.book_ref, bf16[512,512]{1,0:T(8,128)(2,1)S(1)} %bitcast.24, bf16[512,512]{1,0:T(8,128)(2,1)S(1)} %collective-permute-done.rest_1_, ...), custom_call_target="tpu_custom_call" | custom-call | flops 8589934592 | bytes 4194304 | tf_op jit(solution)/shard_map/book_grad/pallas_call | solution.py:286
  108.9 1.6 %reduce_sum.12 = bf16[16,256]{1,0:T(8,128)(2,1)} reduce(bf16[32,16,256]{2,1,0:T(8,128)(2,1)} %all-to-all-done.3, bf16[]{:T(256)} %constant.43.clone.1), dimensions={0}, to_apply=%region_0.0 | reduce | flops 126976 | bytes 270338 | tf_op jit(solution)/shard_map/reduce_sum | solution.py:338
  (14 shorter events, 0.2 us)
Async XLA Ops:
  2.2 28.3 %all-to-all-start = ((bf16[32,16,512]{2,1,0:T(8,128)(2,1)}), bf16[32,16,512]{2,1,0:T(8,128)(2,1)S(1)}, u32[]{:S(2)}, u32[]{:S(2)}) async-start(bf16[32,16,512]{2,1,0:T(8,128)(2,1)} %broadcast_in_dim.6), calls=%async_computation | async-start | bytes 1048576 | tf_op jit(solution)/shard_map/all_to_all | solution.py:315
  41.0 14.0 %collective-permute-start = (bf16[512,512]{1,0:T(8,128)(2,1)S(1)}, bf16[512,512]{1,0:T(8,128)(2,1)S(1)}, u32[]{:S(2)}, u32[]{:S(2)}) collective-permute-start(bf16[512,512]{1,0:T(8,128)(2,1)S(1)} %bitcast.16), channel_id=1, source_target_pairs={{0,64},{64,128},{128,192},{192,0},{1,65},{65,129},{129,193},{193,1... | collective-permute-start | bytes 1572872 | tf_op jit(solution)/shard_map/ppermute | solution.py:331
  42.2 23.3 %collective-permute-start.1 = (bf16[512,512]{1,0:T(8,128)(2,1)S(1)}, bf16[512,512]{1,0:T(8,128)(2,1)S(1)}, u32[]{:S(2)}, u32[]{:S(2)}) collective-permute-start(bf16[512,512]{1,0:T(8,128)(2,1)S(1)} %bitcast.17), channel_id=1, source_target_pairs={{0,128},{64,192},{128,0},{192,64},{1,129},{65,193},{129,1},{193,65... | collective-permute-start | bytes 1572872 | tf_op jit(solution)/shard_map/ppermute | solution.py:331
  44.7 24.1 %collective-permute-start.2 = (bf16[512,512]{1,0:T(8,128)(2,1)S(1)}, bf16[512,512]{1,0:T(8,128)(2,1)S(1)}, u32[]{:S(2)}, u32[]{:S(2)}) collective-permute-start(bf16[512,512]{1,0:T(8,128)(2,1)S(1)} %bitcast.18), channel_id=1, source_target_pairs={{0,192},{64,0},{128,64},{192,128},{1,193},{65,1},{129,65},{193,129... | collective-permute-start | bytes 1572872 | tf_op jit(solution)/shard_map/ppermute | solution.py:331
  45.9 30.5 %all-to-all-start.1 = ((f32[32,4,512]{2,1,0:T(4,128)}), f32[32,4,512]{2,1,0:T(4,128)S(1)}, u32[]{:S(2)}, u32[]{:S(2)}) async-start(f32[32,4,512]{2,1,0:T(4,128)} %get-tuple-element.17), calls=%async_computation.1 | async-start | bytes 524288 | tf_op jit(solution)/shard_map/all_to_all | solution.py:327
  52.2 43.2 %collective-permute-start.3 = (bf16[512,512]{1,0:T(8,128)(2,1)S(1)}, bf16[512,512]{1,0:T(8,128)(2,1)S(1)}, u32[]{:S(2)}, u32[]{:S(2)}) collective-permute-start(bf16[512,512]{1,0:T(8,128)(2,1)S(1)} %bitcast.19), channel_id=1, source_target_pairs={{0,32},{32,0},{1,33},{33,1},{2,34},{34,2},{3,35},{35,3},{4,36},{36... | collective-permute-start | bytes 1572872 | tf_op jit(solution)/shard_map/ppermute | solution.py:343
  55.0 40.5 %collective-permute-start.4 = (bf16[512,512]{1,0:T(8,128)(2,1)S(1)}, bf16[512,512]{1,0:T(8,128)(2,1)}, u32[]{:S(2)}, u32[]{:S(2)}) collective-permute-start(bf16[512,512]{1,0:T(8,128)(2,1)S(1)} %collective-permute-done.rest_1_), channel_id=1, source_target_pairs={{0,32},{32,0},{1,33},{33,1},{2,34},{34,2},{3,35},{35,3},{4,36},{36... | collective-permute-start | bytes 1572872 | tf_op jit(solution)/shard_map/ppermute | solution.py:343
  65.5 30.0 %collective-permute-start.5 = (bf16[512,512]{1,0:T(8,128)(2,1)S(1)}, bf16[512,512]{1,0:T(8,128)(2,1)}, u32[]{:S(2)}, u32[]{:S(2)}) collective-permute-start(bf16[512,512]{1,0:T(8,128)(2,1)S(1)} %collective-permute-done.1.rest_2_), channel_id=1, source_target_pairs={{0,32},{32,0},{1,33},{33,1},{2,34},{34,2},{3,35},{35,3},{4,36},{36... | collective-permute-start | bytes 1572872 | tf_op jit(solution)/shard_map/ppermute | solution.py:343
  68.8 26.7 %collective-permute-start.6 = (bf16[512,512]{1,0:T(8,128)(2,1)S(1)}, bf16[512,512]{1,0:T(8,128)(2,1)}, u32[]{:S(2)}, u32[]{:S(2)}) collective-permute-start(bf16[512,512]{1,0:T(8,128)(2,1)S(1)} %collective-permute-done.2.rest_3_), channel_id=1, source_target_pairs={{0,32},{32,0},{1,33},{33,1},{2,34},{34,2},{3,35},{35,3},{4,36},{36... | collective-permute-start | bytes 1572872 | tf_op jit(solution)/shard_map/ppermute | solution.py:343
  68.8 7.7 %copy-start = (s32[512]{0:T(512)S(1)}, s32[512]{0:T(512)}, u32[]{:S(2)}) copy-start(s32[512]{0:T(512)} %param.6) | copy-start | bytes 6148
  77.2 12.9 %all-to-all-start.2 = ((f32[8,4,512]{2,1,0:T(4,128)}), f32[8,4,512]{2,1,0:T(4,128)S(1)}, u32[]{:S(2)}, u32[]{:S(2)}) async-start(f32[8,4,512]{2,1,0:T(4,128)} %get-tuple-element.18.all_ref), calls=%async_computation.2 | async-start | bytes 131072 | tf_op jit(solution)/shard_map/all_to_all | solution.py:334
  90.1 18.8 %all-to-all-start.3 = ((bf16[32,16,256]{2,1,0:T(8,128)(2,1)}), bf16[32,16,256]{2,1,0:T(8,128)(2,1)}, u32[]{:S(2)}, u32[]{:S(2)}) async-start(bf16[32,16,256]{2,1,0:T(8,128)(2,1)} %bitcast.2), calls=%async_computation.3 | async-start | bytes 524288 | tf_op jit(solution)/shard_map/all_to_all | solution.py:337
where the time goes:
time: 111 us
  Pallas kernels  48.3 us (44%)
  starting transfers between devices  41 us (37%)
  waiting for transfers between devices  14.8 us (13%)
  other arithmetic  3.01 us (3%)
  local copies, waits for them, and re-layouts  2.73 us (2%)
    pallas_call x1, Pallas kernels, book_grad(): pl.pallas_call(functools.partial(book_kernel, groups), grid_spec=grid_spe...  13.4 us
    all_to_all x1, starting transfers between devices, per_device(): lax.all_to_all(jnp.broadcast_to(both[None], (peers, own_count, 2 * d)), Z...  12 us
    pallas_call x1, Pallas kernels, local_stats(): pl.pallas_call(functools.partial(stats_kernel, steps), grid=(steps,), in_...  10.5 us
    ppermute x4, starting transfers between devices, per_device(): other.append(lax.ppermute(piece, 'core', swap))  9.5 us
    pallas_call x1, Pallas kernels, lat_second(): pl.pallas_call(functools.partial(second_kernel, steps), grid=(steps,), in...  8.26 us
    pallas_call x1, Pallas kernels, pick_rows(): pl.pallas_call(functools.partial(pick_kernel, cb), grid=(codes // cb,), i...  7.73 us
    all_to_all x1, waiting for transfers between devices, per_device(): lax.all_to_all(jnp.broadcast_to(both[None], (peers, own_count, 2 * d)), Z...  7.73 us
    pallas_call x1, Pallas kernels, lat_first(): pl.pallas_call(first_kernel, grid=(codes // cb // 2,), in_specs=lat_specs...  7.66 us
  transfers between devices with their start and end apart: 11, of which 2 were waited for; matrix products, arithmetic and copies ran while one was open for 2% of the time, Pallas kernels for 34%

commit v1 on v0

--- a/solution.py
+++ b/solution.py
@@ -45,7 +45,7 @@
 
 def pick_rows(tgt_cols, book):
     tokens, codes, d = tgt_cols.shape[0], *book.shape
-    cb = 1024
+    cb = 2048
     return pl.pallas_call(
         functools.partial(pick_kernel, cb),
         grid=(codes // cb,),
@@ -61,7 +61,19 @@
     )(tgt_cols, book)
 
 
-def stats_kernel(steps, lat_ref, grad_ref, rows_ref, book_ref, out_ref, m_col, mean_col, m_s, l_s, w_s):
+def fold(x):
+    return sum(x[:, i : i + 128] for i in range(0, x.shape[1], 128))
+
+
+def as_row(x):
+    return jnp.sum(x.T, axis=0, keepdims=True)
+
+
+def as_cols(row):
+    return jnp.broadcast_to(row, (128, row.shape[1])).T
+
+
+def stats_kernel(steps, sub, lat_ref, grad_ref, rows_ref, book_ref, out_ref, m_col, mean_col, m_s, l_s, w_s):
     i = pl.program_id(0)
 
     @pl.when(i == 0)
@@ -70,17 +82,26 @@
         l_s[...] = jnp.zeros_like(l_s)
         w_s[...] = jnp.zeros_like(w_s)
 
-    block = book_ref[...]
-    cb, tokens = block.shape[0], lat_ref.shape[0]
-    logit = dot(block, lat_ref[...], NT).reshape(cb // 8, 8, tokens)
-    back = dot(block, grad_ref[...], NT).reshape(cb // 8, 8, tokens)
-    old = m_s[...]
-    new = jnp.maximum(old, jnp.max(logit, axis=0))
-    factor = jnp.exp(old - new)
-    expo = jnp.exp(logit - new[None])
-    l_s[...] = l_s[...] * factor + jnp.sum(expo, axis=0)
-    w_s[...] = w_s[...] * factor + jnp.sum(expo * back, axis=0)
-    m_s[...] = new
+    cb, tokens = book_ref.shape[0], lat_ref.shape[0]
+    count = cb // sub
+
+    def scores(ref, j):
+        return dot(book_ref[j * sub : (j + 1) * sub, :], ref[...], NT).reshape(sub // 8, 8, tokens)
+
+    m, l, w = m_s[...], l_s[...], w_s[...]
+    ahead = scores(lat_ref, 0)
+    for j in range(count):
+        logit = ahead
+        if j + 1 < count:
+            ahead = scores(lat_ref, j + 1)
+        back = scores(grad_ref, j)
+        new = jnp.maximum(m, jnp.max(logit, axis=0))
+        factor = jnp.exp(m - new)
+        expo = jnp.exp(logit - new[None])
+        l = l * factor + jnp.sum(expo, axis=0)
+        w = w * factor + jnp.sum(expo * back, axis=0)
+        m = new
+    m_s[...], l_s[...], w_s[...] = m, l, w
 
     @pl.when(i == steps - 1)
     def _():
@@ -89,20 +110,19 @@
         scale = jnp.exp(m - top)
         total = jnp.sum(l_s[...] * scale, axis=0, keepdims=True)
         weighted = jnp.sum(w_s[...] * scale, axis=0, keepdims=True)
-        prod = lat_ref[...].astype(F32) * rows_ref[...]
-        picked = dot(jnp.ones((8, prod.shape[1]), F32), prod, NT, lax.Precision.HIGHEST)[:1]
+        picked = as_row(fold(lat_ref[...].astype(F32) * rows_ref[...]))
         pack = jnp.concatenate([top, total, weighted, picked], axis=0)
         out_ref[...] = jnp.broadcast_to(pack[None], out_ref.shape)
-        m_col[...] = jnp.broadcast_to(top, (128, tokens)).T
-        mean_col[...] = jnp.broadcast_to(weighted / total, (128, tokens)).T
-
-
-def local_stats(toks, rows, book, peers):
+        m_col[...] = as_cols(top)
+        mean_col[...] = as_cols(weighted / total)
+
+
+def local_stats(toks, rows, book, peers, cb=4096, sub=512):
     tokens, (codes, d) = toks.shape[0], book.shape
-    cb = 1024
     steps = codes // cb
-    return pl.pallas_call(
-        functools.partial(stats_kernel, steps),
+    cols = pl.BlockSpec((tokens, 128), lambda i: (0, 0))
+    return pl.pallas_call(
+        functools.partial(stats_kernel, steps, sub),
         grid=(steps,),
         in_specs=[
             pl.BlockSpec((tokens, d), lambda i: (0, 0)),
@@ -110,11 +130,7 @@
             pl.BlockSpec((tokens, d), lambda i: (0, 0)),
             pl.BlockSpec((cb, d), lambda i: (i, 0)),
         ],
-        out_specs=[
-            pl.BlockSpec((peers, 4, tokens), lambda i: (0, 0, 0)),
-            pl.BlockSpec((tokens, 128), lambda i: (0, 0)),
-            pl.BlockSpec((tokens, 128), lambda i: (0, 0)),
-        ],
+        out_specs=[pl.BlockSpec((peers, 4, tokens), lambda i: (0, 0, 0)), cols, cols],
         out_shape=[
             jax.ShapeDtypeStruct((peers, 4, tokens), F32),
             pltpu.HBM((tokens, 128), F32),
@@ -127,44 +143,57 @@
     )(toks, toks, rows, book)
 
 
-def lat_step(lat_ref, grad_ref, m_ref, mean_ref, book_ref, a_ref, b_ref):
-    block = book_ref[...]
-    logit = dot(lat_ref[...], block, NT)
-    back = dot(grad_ref[...], block, NT)
-    expo = jnp.exp(logit - m_ref[:, :1])
-    dev = expo * (back - mean_ref[:, :1])
-    a_ref[...] += dot(dev.astype(BF16), block, NN)
-    b_ref[...] += dot(expo.astype(BF16), block, NN)
-
-
-def first_kernel(lat_ref, grad_ref, m_ref, mean_ref, book_ref, a_ref, b_ref):
+def lat_step(sub, lat_ref, grad_ref, m_ref, book_ref, outs, weigh):
+    count = book_ref.shape[0] // sub
+
+    def block(j):
+        return book_ref[j * sub : (j + 1) * sub, :]
+
+    sums = [ref[...] for ref in outs]
+    ahead = dot(lat_ref[...], block(0), NT)
+    for j in range(count):
+        logit = ahead
+        if j + 1 < count:
+            ahead = dot(lat_ref[...], block(j + 1), NT)
+        back = dot(grad_ref[...], block(j), NT)
+        terms = weigh(jnp.exp(logit - m_ref[:, :1]), back)
+        sums = [x + dot(term.astype(BF16), block(j), NN) for x, term in zip(sums, terms)]
+    for ref, x in zip(outs, sums):
+        ref[...] = x
+
+
+def first_kernel(sub, lat_ref, grad_ref, m_ref, mean_ref, book_ref, a_ref, b_ref):
     @pl.when(pl.program_id(0) == 0)
     def _():
         a_ref[...] = jnp.zeros_like(a_ref)
         b_ref[...] = jnp.zeros_like(b_ref)
 
-    lat_step(lat_ref, grad_ref, m_ref, mean_ref, book_ref, a_ref, b_ref)
+    def weigh(expo, back):
+        return expo * (back - mean_ref[:, :1]), expo
+
+    lat_step(sub, lat_ref, grad_ref, m_ref, book_ref, (a_ref, b_ref), weigh)
 
 
 def second_kernel(
-    steps, lat_ref, grad_ref, m_ref, mean_ref, book_ref, a0, b0, rows_ref, all_ref, part_ref, a_ref, b_ref
+    steps, sub, lat_ref, grad_ref, m_ref, mean_ref, book_ref, a0, b0, rows_ref, all_ref,
+    part_ref, sum_ref, lse_col, mean_col,
 ):
     @pl.when(pl.program_id(0) == 0)
     def _():
-        a_ref[...] = a0[...]
-        b_ref[...] = b0[...]
-
-    lat_step(lat_ref, grad_ref, m_ref, mean_ref, book_ref, a_ref, b_ref)
+        lse_col[...] = as_cols(all_ref[0, 0:1, :])
+        mean_col[...] = as_cols(all_ref[0, 1:2, :])
+        own = jnp.exp(m_ref[...] - lse_col[...])
+        ratio = own * (ce_weight + mean_ref[...] - mean_col[...])
+        sum_ref[...] = own[:, :1] * a0[...] + ratio[:, :1] * b0[...] - ce_weight * rows_ref[...]
+
+    def weigh(prob, back):
+        return (prob * (back - mean_col[:, :1]) + ce_weight * prob,)
+
+    lat_step(sub, lat_ref, grad_ref, lse_col, book_ref, (sum_ref,), weigh)
 
     @pl.when(pl.program_id(0) == steps - 1)
     def _():
-        tokens = m_ref.shape[0]
-        lse = jnp.broadcast_to(all_ref[0, 0:1, :], (128, tokens)).T
-        mean = jnp.broadcast_to(all_ref[0, 1:2, :], (128, tokens)).T
-        own = jnp.exp(m_ref[...] - lse)
-        ratio = own * (ce_weight + mean_ref[...] - mean)
-        part = own[:, :1] * a_ref[...] + ratio[:, :1] * b_ref[...] - ce_weight * rows_ref[...]
-        part_ref[...] = part.astype(part_ref.dtype)
+        part_ref[...] = sum_ref[...].astype(part_ref.dtype)
 
 
 def lat_specs(tokens, d, cb, first):
@@ -177,38 +206,38 @@
     ]
 
 
-def lat_first(toks, m_col, mean_col, book):
+def lat_first(toks, m_col, mean_col, book, part=1, parts=2, cb=4096, sub=512):
     tokens, (codes, d) = toks.shape[0], book.shape
-    cb = 1024
+    steps = codes // cb * part // parts
     whole = pl.BlockSpec((tokens, d), lambda i: (0, 0))
     return pl.pallas_call(
-        first_kernel,
-        grid=(codes // cb // 2,),
+        functools.partial(first_kernel, sub),
+        grid=(steps,),
         in_specs=lat_specs(tokens, d, cb, 0),
         out_specs=[whole] * 2,
         out_shape=[pltpu.HBM((tokens, d), F32)] * 2,
         compiler_params=params(),
-        cost_estimate=cost(4 * tokens * codes * d, codes * d, tokens * codes // 2),
+        cost_estimate=cost(8 * tokens * cb * steps * d, cb * steps * d * 2, tokens * cb * steps),
         name="lat_first",
     )(toks, toks, m_col, mean_col, book)
 
 
-def lat_second(toks, m_col, mean_col, book, a, b, rows, row):
+def lat_second(toks, m_col, mean_col, book, a, b, rows, row, part=1, parts=2, cb=4096, sub=512):
     tokens, (codes, d) = toks.shape[0], book.shape
-    cb = 1024
-    steps = codes // cb // 2
+    first = codes // cb * part // parts
+    steps = codes // cb - first
     whole = pl.BlockSpec((tokens, d), lambda i: (0, 0))
     return pl.pallas_call(
-        functools.partial(second_kernel, steps),
+        functools.partial(second_kernel, steps, sub),
         grid=(steps,),
-        in_specs=lat_specs(tokens, d, cb, steps)
+        in_specs=lat_specs(tokens, d, cb, first)
         + [whole] * 3
         + [pl.BlockSpec((1, 4, tokens), lambda i: (0, 0, 0))],
         out_specs=whole,
         out_shape=jax.ShapeDtypeStruct((tokens, d), BF16),
-        scratch_shapes=[pltpu.VMEM((tokens, d), F32)] * 2,
-        compiler_params=params(),
-        cost_estimate=cost(4 * tokens * codes * d, codes * d, tokens * codes // 2),
+        scratch_shapes=[pltpu.VMEM((tokens, d), F32)] + [pltpu.VMEM((tokens, 128), F32)] * 2,
+        compiler_params=params(),
+        cost_estimate=cost(6 * tokens * cb * steps * d, cb * steps * d * 2, tokens * cb * steps),
         name="lat_second",
     )(toks, toks, m_col, mean_col, book, a, b, rows, row)
 
@@ -240,59 +269,70 @@
     )(stats, tgt)
 
 
-def book_kernel(groups, s_ref, rows_ref, book_ref, *rest):
+def book_kernel(first, sub, s_ref, rows_ref, book_ref, *rest):
+    start, rest = (rest[:1], rest[1:]) if first else ((), rest)
+    groups = len(rest) - 3
     toks, (out_ref, buf, sem) = rest[:groups], rest[groups:]
     for g in range(groups):
         pltpu.make_async_copy(toks[g], buf.at[g], sem.at[g]).start()
-    block = book_ref[...]
-    cb, d = block.shape
-    out_ref[...] = jnp.zeros_like(out_ref)
-
-    def step(g, carry):
-        pltpu.make_async_copy(toks[0], buf.at[g], sem.at[g]).wait()
-        row = rows_ref[s_ref[g]]
-        tokens = row.shape[1]
-        both = buf[g]
-        lat, grad = both[:, :d], both[:, d:]
-        logit = dot(block, lat, NT)
-        back = dot(block, grad, NT)
+    chunk, d = book_ref.shape
+    tokens = buf.shape[1]
+    ids = lax.broadcasted_iota(jnp.int32, (sub, tokens), 0) + s_ref[s_ref.shape[0] - 1]
+    work = [(g, j) for g in range(groups) for j in range(chunk // sub)]
+
+    def block(j):
+        return book_ref[j * sub : (j + 1) * sub, :]
+
+    def logits(g, j):
+        if j == 0:
+            pltpu.make_async_copy(toks[g], buf.at[g], sem.at[g]).wait()
+        return dot(block(j), buf[g, :, :d], NT)
+
+    ahead = logits(*work[0])
+    for n, (g, j) in enumerate(work):
+        logit = ahead
+        if n + 1 < len(work):
+            ahead = logits(*work[n + 1])
+        row = rows_ref[s_ref[first + g]]
+        back = dot(block(j), buf[g, :, d:], NT)
         prob = jnp.exp(logit - row[0:1])
-        ids = lax.broadcasted_iota(jnp.int32, (cb, tokens), 0)
-        hit = jnp.where(ids == row[2:3].astype(jnp.int32) - s_ref[groups], 1.0, 0.0)
+        hit = jnp.where(ids + j * sub == row[2:3].astype(jnp.int32), 1.0, 0.0)
         delta = prob * (back - row[1:2]) + ce_weight * (prob - hit)
-        out_ref[...] += dot(delta.astype(BF16), lat, NN) + dot(hit.astype(BF16), grad, NN)
-        return carry
-
-    lax.fori_loop(0, groups, step, 0)
-
-
-def book_grad(scalars, rows, book, toks):
+        out = dot(delta.astype(BF16), buf[g, :, :d], NN) + dot(hit.astype(BF16), buf[g, :, d:], NN)
+        at = slice(j * sub, (j + 1) * sub)
+        if g == 0 and not start:
+            out_ref[at, :] = out
+        else:
+            out_ref[at, :] = (start[0] if g == 0 else out_ref)[at, :] + out
+
+
+def book_grad(scalars, rows, book, toks, start=None, sub=512):
     groups = len(toks)
     (tokens, width), (chunk, d) = toks[0].shape, book.shape
+    whole = pl.BlockSpec((chunk, d), lambda i, s: (0, 0))
+    extra = [] if start is None else [start]
     grid_spec = pltpu.PrefetchScalarGridSpec(
         num_scalar_prefetch=1,
         grid=(1,),
-        in_specs=[
-            pl.BlockSpec((groups, 4, tokens), lambda i, s: (0, 0, 0)),
-            pl.BlockSpec((chunk, d), lambda i, s: (0, 0)),
-        ]
+        in_specs=[pl.BlockSpec(rows.shape, lambda i, s: (0, 0, 0)), whole]
+        + [whole for _ in extra]
         + [pl.BlockSpec(memory_space=pl.ANY)] * groups,
-        out_specs=pl.BlockSpec((chunk, d), lambda i, s: (0, 0)),
+        out_specs=whole,
         scratch_shapes=[
             pltpu.VMEM((groups, tokens, width), BF16),
             pltpu.SemaphoreType.DMA((groups,)),
         ],
     )
     return pl.pallas_call(
-        functools.partial(book_kernel, groups),
+        functools.partial(book_kernel, 0 if start is None else groups, sub),
         grid_spec=grid_spec,
         out_shape=jax.ShapeDtypeStruct((chunk, d), F32),
         compiler_params=params(),
         cost_estimate=cost(
             8 * groups * tokens * chunk * d, groups * tokens * width * 2, groups * tokens * chunk
         ),
-        name="book_grad",
-    )(scalars, rows, book, *toks)
+        name="book_first" if start is None else "book_second",
+    )(scalars, rows, book, *extra, *toks)
 
 
 def in_hbm(*arrays):
@@ -341,7 +381,8 @@
     other = []
     for piece in same:
         other.append(lax.ppermute(piece, "core", swap))
-    codebook_grad = book_grad(scalars, everyone, own_book, same + other)
+    half = book_grad(scalars, everyone, own_book, same)
+    codebook_grad = book_grad(scalars, everyone, own_book, other, half)
     return latent_grad, codebook_grad, token_loss
 
 

time: 111 us -> 105 us (0.946)
  Pallas kernels: 48.3 us -> 42.5 us
    all_to_all x1, starting transfers between devices: 5.38 us -> 9.57 us  [per_device(): moved = lax.all_to_all(part.reshape(peers, own_count, d), ZY, 0, 0)]
    pallas_call x4 -> x5, Pallas kernels: 39.8 us -> 36.1 us  [the longest x2 14.2 us: book_grad(): pl.pallas_call(functools.partial(book_kernel, 0 if start is None else gro...]
    ppermute x4, starting transfers between devices: 9.5 us -> 6.1 us  [per_device(): other.append(lax.ppermute(piece, 'core', swap))]
    ppermute x3, waiting for transfers between devices: 7.02 us -> 4.71 us  [per_device(): same.append(lax.ppermute(late, 'x', [(i, (i + k) % nx) for i in range(nx)]))]
    pallas_call x1, Pallas kernels: 7.73 us -> 5.65 us  [pick_rows(): pl.pallas_call(functools.partial(pick_kernel, cb), grid=(codes // cb,), i...]
    all_to_all x1, waiting for transfers between devices: 7.73 us -> 9.7 us  [per_device(): lax.all_to_all(jnp.broadcast_to(both[None], (peers, own_count, 2 * d)), Z...]
  transfers between devices with their start and end apart: 11 -> 11, of which waited for: 2 -> 2; matrix products, arithmetic and copies ran while one was open for 2% -> 2% of each run, Pallas kernels for 34% -> 33%
where the time goes in v1:
time: 105 us
  Pallas kernels  42.5 us (40%)
  starting transfers between devices  41.1 us (39%)
  waiting for transfers between devices  14.4 us (14%)
  other arithmetic  3.01 us (3%)
  local copies, waits for them, and re-layouts  2.72 us (3%)
    pallas_call x2, Pallas kernels, book_grad(): pl.pallas_call(functools.partial(book_kernel, 0 if start is None else gro...  14.2 us
    all_to_all x1, starting transfers between devices, per_device(): lax.all_to_all(jnp.broadcast_to(both[None], (peers, own_count, 2 * d)), Z...  12 us
    all_to_all x1, waiting for transfers between devices, per_device(): lax.all_to_all(jnp.broadcast_to(both[None], (peers, own_count, 2 * d)), Z...  9.7 us
    all_to_all x1, starting transfers between devices, per_device(): moved = lax.all_to_all(part.reshape(peers, own_count, d), ZY, 0, 0)  9.57 us
    pallas_call x1, Pallas kernels, local_stats(): pl.pallas_call(functools.partial(stats_kernel, steps, sub), grid=(steps,)...  8.03 us
    pallas_call x1, Pallas kernels, lat_first(): pl.pallas_call(functools.partial(first_kernel, sub), grid=(steps,), in_sp...  7.35 us
    pallas_call x1, Pallas kernels, lat_second(): pl.pallas_call(functools.partial(second_kernel, steps, sub), grid=(steps,...  6.53 us
    ppermute x4, starting transfers between devices, per_device(): other.append(lax.ppermute(piece, 'core', swap))  6.1 us
  transfers between devices with their start and end apart: 11, of which 2 were waited for; matrix products, arithmetic and copies ran while one was open for 2% of the time, Pallas kernels for 33%

profile of v1, /device:TPU:1, one launch (start us, length us, event | category | flops | bytes accessed | tf_op | source)
XLA Modules:
  0.0 104.6 jit_solution(9612850480081210882)
XLA Ops:
  0.6 0.7 pad_maximum_fusion
  1.3 0.9 broadcast_in_dim.6
  2.2 12.0 %all-to-all-start = ((bf16[32,16,512]{2,1,0:T(8,128)(2,1)}), bf16[32,16,512]{2,1,0:T(8,128)(2,1)S(1)}, u32[]{:S(2)}, u32[]{:S(2)}) async-start(bf16[32,16,512]{2,1,0:T(8,128)(2,1)} %broadcast_in_dim.6), calls=%async_computation | async-start | bytes 1048576 | tf_op jit(solution)/shard_map/all_to_all | solution.py:355
  14.3 0.7 broadcast_subtract_fusion
  15.2 5.7 %pick.1.rows_ref = f32[512,256]{1,0:T(8,128)} custom-call(s32[512,128]{1,0:T(8,128)S(1)} %broadcast_in_dim.7.tgt_ref, bf16[8192,256]{1,0:T(8,128)(2,1)} %book_ref.7), custom_call_target="tpu_custom_call" | custom-call | flops 2147483648 | bytes 4194304 | tf_op jit(solution)/shard_map/pick/pallas_call | solution.py:49
  20.8 9.7 %all-to-all-done = bf16[32,16,512]{2,1,0:T(8,128)(2,1)S(1)} async-done(((bf16[32,16,512]{2,1,0:T(8,128)(2,1)}), bf16[32,16,512]{2,1,0:T(8,128)(2,1)S(1)}, u32[]{:S(2)}, u32[]{:S(2)}) %all-to-all-start) | async-done | bytes 524320 | tf_op jit(solution)/shard_map/all_to_all | solution.py:355
  30.5 8.0 %stats.1 = (f32[32,4,512]{2,1,0:T(4,128)}, f32[512,128]{1,0:T(8,128)}, f32[512,128]{1,0:T(8,128)}) custom-call(bf16[512,512]{1,0:T(8,128)(2,1)S(1)} %bitcast.14, bf16[512,512]{1,0:T(8,128)(2,1)S(1)} %bitcast.15, f32[512,256]{1,0:T(8,128)} %pick.1.rows_ref, bf16[8192,256]{1,0:T(8,128)(2,1)} %book_ref.7), custom_call_target="tpu_custom_call" | custom-call | flops 4294967296 | bytes 4194304 | tf_op jit(solution)/shard_map/stats/pallas_call | solution.py:124
  38.6 5.3 %all-to-all-start.1 = ((f32[32,4,512]{2,1,0:T(4,128)}), f32[32,4,512]{2,1,0:T(4,128)S(1)}, u32[]{:S(2)}, u32[]{:S(2)}) async-start(f32[32,4,512]{2,1,0:T(4,128)} %get-tuple-element.17), calls=%async_computation.1 | async-start | bytes 524288 | tf_op jit(solution)/shard_map/all_to_all | solution.py:367
  43.8 1.3 %collective-permute-start = (bf16[512,512]{1,0:T(8,128)(2,1)S(1)}, bf16[512,512]{1,0:T(8,128)(2,1)S(1)}, u32[]{:S(2)}, u32[]{:S(2)}) collective-permute-start(bf16[512,512]{1,0:T(8,128)(2,1)S(1)} %bitcast.16), channel_id=1, source_target_pairs={{0,64},{64,128},{128,192},{192,0},{1,65},{65,129},{129,193},{193,1... | collective-permute-start | bytes 1572872 | tf_op jit(solution)/shard_map/ppermute | solution.py:371
  45.1 2.5 %collective-permute-start.1 = (bf16[512,512]{1,0:T(8,128)(2,1)S(1)}, bf16[512,512]{1,0:T(8,128)(2,1)S(1)}, u32[]{:S(2)}, u32[]{:S(2)}) collective-permute-start(bf16[512,512]{1,0:T(8,128)(2,1)S(1)} %bitcast.17), channel_id=1, source_target_pairs={{0,128},{64,192},{128,0},{192,64},{1,129},{65,193},{129,1},{193,65... | collective-permute-start | bytes 1572872 | tf_op jit(solution)/shard_map/ppermute | solution.py:371
  47.6 1.2 %collective-permute-start.2 = (bf16[512,512]{1,0:T(8,128)(2,1)S(1)}, bf16[512,512]{1,0:T(8,128)(2,1)S(1)}, u32[]{:S(2)}, u32[]{:S(2)}) collective-permute-start(bf16[512,512]{1,0:T(8,128)(2,1)S(1)} %bitcast.18), channel_id=1, source_target_pairs={{0,192},{64,0},{128,64},{192,128},{1,193},{65,1},{129,65},{193,129... | collective-permute-start | bytes 1572872 | tf_op jit(solution)/shard_map/ppermute | solution.py:371
  48.7 1.1 %constant_dynamic-slice_fusion.book_ref = bf16[1024,256]{1,0:T(8,128)(2,1)S(1)} fusion(bf16[8192,256]{1,0:T(8,128)(2,1)} %book_ref.7, s32[]{:T(128)S(6)} %select_n.6), kind=kLoop, calls=%fused_computation.3 | loop fusion | bytes 1048580 | tf_op jit(solution)/shard_map/dynamic_slice | solution.py:364
  49.8 2.7 %collective-permute-start.3 = (bf16[512,512]{1,0:T(8,128)(2,1)S(1)}, bf16[512,512]{1,0:T(8,128)(2,1)S(1)}, u32[]{:S(2)}, u32[]{:S(2)}) collective-permute-start(bf16[512,512]{1,0:T(8,128)(2,1)S(1)} %bitcast.19), channel_id=1, source_target_pairs={{0,32},{32,0},{1,33},{33,1},{2,34},{34,2},{3,35},{35,3},{4,36},{36... | collective-permute-start | bytes 1572872 | tf_op jit(solution)/shard_map/ppermute | solution.py:383
  52.5 7.4 %lat_first.1 = (f32[512,256]{1,0:T(8,128)}, f32[512,256]{1,0:T(8,128)}) custom-call(bf16[512,512]{1,0:T(8,128)(2,1)S(1)} %bitcast.20, bf16[512,512]{1,0:T(8,128)(2,1)S(1)} %bitcast.21, f32[512,128]{1,0:T(8,128)} %get-tuple-element.13.m_ref, f32[512,128]{1,0:T(8,128)} %get-tuple-element.14.mean_ref, bf16[8192,256]{1,0:T(8,128)(2,1)} %book_ref.7), custom_call_target="tpu_custom_call" | custom-call | flops 4294967296 | bytes 2097152 | tf_op jit(solution)/shard_map/lat_first/pallas_call | solution.py:213
  59.9 0.7 combine.1
  60.6 3.3 %all-to-all-start.2 = ((f32[8,4,512]{2,1,0:T(4,128)}), f32[8,4,512]{2,1,0:T(4,128)S(1)}, u32[]{:S(2)}, u32[]{:S(2)}) async-start(f32[8,4,512]{2,1,0:T(4,128)} %get-tuple-element.18.all_ref), calls=%async_computation.2 | async-start | bytes 131072 | tf_op jit(solution)/shard_map/all_to_all | solution.py:374
  64.3 4.7 %collective-permute-done.1.rest_2_ = bf16[512,512]{1,0:T(8,128)(2,1)S(1)} collective-permute-done((bf16[512,512]{1,0:T(8,128)(2,1)S(1)}, bf16[512,512]{1,0:T(8,128)(2,1)S(1)}, u32[]{:S(2)}, u32[]{:S(2)}) %collective-permute-start.1) | collective-permute-done | bytes 524320 | tf_op jit(solution)/shard_map/ppermute | solution.py:371
  69.0 3.0 %collective-permute-start.5 = (bf16[512,512]{1,0:T(8,128)(2,1)S(1)}, bf16[512,512]{1,0:T(8,128)(2,1)}, u32[]{:S(2)}, u32[]{:S(2)}) collective-permute-start(bf16[512,512]{1,0:T(8,128)(2,1)S(1)} %collective-permute-done.1.rest_2_), channel_id=1, source_target_pairs={{0,32},{32,0},{1,33},{33,1},{2,34},{34,2},{3,35},{35,3},{4,36},{36... | collective-permute-start | bytes 1572872 | tf_op jit(solution)/shard_map/ppermute | solution.py:383
  72.0 6.5 %lat_second.1 = bf16[512,256]{1,0:T(8,128)(2,1)} custom-call(bf16[512,512]{1,0:T(8,128)(2,1)S(1)} %bitcast.22, bf16[512,512]{1,0:T(8,128)(2,1)S(1)} %bitcast.23, f32[512,128]{1,0:T(8,128)} %get-tuple-element.13.m_ref, f32[512,128]{1,0:T(8,128)} %get-tuple-element.14.mean_ref, bf16[8192,256]{1,0:T(8,128)(2,1)} %book_ref.7, f32[512,256]{1,0:T(8,128)} %get-tuple-element.15.a0, ...), custom_call_target="tpu_custom_call" | custom-call | flops 3221225472 | bytes 2097152 | tf_op jit(solution)/shard_map/lat_second/pallas_call | solution.py:230
  78.5 0.6 dynamic-slice_bitcast_fusion
  79.1 9.6 %all-to-all-start.3 = ((bf16[32,16,256]{2,1,0:T(8,128)(2,1)}), bf16[32,16,256]{2,1,0:T(8,128)(2,1)}, u32[]{:S(2)}, u32[]{:S(2)}) async-start(bf16[32,16,256]{2,1,0:T(8,128)(2,1)} %bitcast.2), calls=%async_computation.3 | async-start | bytes 524288 | tf_op jit(solution)/shard_map/all_to_all | solution.py:377
  88.7 6.6 %book_first.1.rest_0_ = f32[1024,256]{1,0:T(8,128)S(1)} custom-call(s32[9]{0:T(128)S(1)} %stack.39.s_ref, f32[8,4,512]{2,1,0:T(4,128)S(1)} %all-to-all-done.2.rows_ref, bf16[1024,256]{1,0:T(8,128)(2,1)S(1)} %constant_dynamic-slice_fusion.book_ref, bf16[512,512]{1,0:T(8,128)(2,1)S(1)} %bitcast.24, bf16[512,512]{1,0:T(8,128)(2,1)S(1)} %collective-permute-done.rest_1_, ...), custom_call_target="tpu_custom_call" | custom-call | flops 4294967296 | bytes 2097152 | tf_op jit(solution)/shard_map/book_first/pallas_call | solution.py:326
  95.4 7.6 %book_second.1 = f32[1024,256]{1,0:T(8,128)} custom-call(s32[9]{0:T(128)S(1)} %stack.39.s_ref, f32[8,4,512]{2,1,0:T(4,128)S(1)} %all-to-all-done.2.rows_ref, bf16[1024,256]{1,0:T(8,128)(2,1)S(1)} %constant_dynamic-slice_fusion.book_ref, f32[1024,256]{1,0:T(8,128)S(1)} %book_first.1.rest_0_, bf16[512,512]{1,0:T(8,128)(2,1)S(1)} %collective-permute-done.3.rest_1_, ...), custom_call_target="tpu_custom_call" | custom-call | flops 4294967296 | bytes 2097152 | tf_op jit(solution)/shard_map/book_second/pallas_call | solution.py:326
  103.0 1.6 %reduce_sum.12 = bf16[16,256]{1,0:T(8,128)(2,1)} reduce(bf16[32,16,256]{2,1,0:T(8,128)(2,1)} %all-to-all-done.3, bf16[]{:T(256)} %constant.43.clone.1), dimensions={0}, to_apply=%region_0.0 | reduce | flops 126976 | bytes 270338 | tf_op jit(solution)/shard_map/reduce_sum | solution.py:378
  (15 shorter events, 0.6 us)
Async XLA Ops:
  2.2 28.3 %all-to-all-start = ((bf16[32,16,512]{2,1,0:T(8,128)(2,1)}), bf16[32,16,512]{2,1,0:T(8,128)(2,1)S(1)}, u32[]{:S(2)}, u32[]{:S(2)}) async-start(bf16[32,16,512]{2,1,0:T(8,128)(2,1)} %broadcast_in_dim.6), calls=%async_computation | async-start | bytes 1048576 | tf_op jit(solution)/shard_map/all_to_all | solution.py:355
  38.6 21.3 %all-to-all-start.1 = ((f32[32,4,512]{2,1,0:T(4,128)}), f32[32,4,512]{2,1,0:T(4,128)S(1)}, u32[]{:S(2)}, u32[]{:S(2)}) async-start(f32[32,4,512]{2,1,0:T(4,128)} %get-tuple-element.17), calls=%async_computation.1 | async-start | bytes 524288 | tf_op jit(solution)/shard_map/all_to_all | solution.py:367
  43.8 20.1 %collective-permute-start = (bf16[512,512]{1,0:T(8,128)(2,1)S(1)}, bf16[512,512]{1,0:T(8,128)(2,1)S(1)}, u32[]{:S(2)}, u32[]{:S(2)}) collective-permute-start(bf16[512,512]{1,0:T(8,128)(2,1)S(1)} %bitcast.16), channel_id=1, source_target_pairs={{0,64},{64,128},{128,192},{192,0},{1,65},{65,129},{129,193},{193,1... | collective-permute-start | bytes 1572872 | tf_op jit(solution)/shard_map/ppermute | solution.py:371
  45.1 23.9 %collective-permute-start.1 = (bf16[512,512]{1,0:T(8,128)(2,1)S(1)}, bf16[512,512]{1,0:T(8,128)(2,1)S(1)}, u32[]{:S(2)}, u32[]{:S(2)}) collective-permute-start(bf16[512,512]{1,0:T(8,128)(2,1)S(1)} %bitcast.17), channel_id=1, source_target_pairs={{0,128},{64,192},{128,0},{192,64},{1,129},{65,193},{129,1},{193,65... | collective-permute-start | bytes 1572872 | tf_op jit(solution)/shard_map/ppermute | solution.py:371
  47.6 24.5 %collective-permute-start.2 = (bf16[512,512]{1,0:T(8,128)(2,1)S(1)}, bf16[512,512]{1,0:T(8,128)(2,1)S(1)}, u32[]{:S(2)}, u32[]{:S(2)}) collective-permute-start(bf16[512,512]{1,0:T(8,128)(2,1)S(1)} %bitcast.18), channel_id=1, source_target_pairs={{0,192},{64,0},{128,64},{192,128},{1,193},{65,1},{129,65},{193,129... | collective-permute-start | bytes 1572872 | tf_op jit(solution)/shard_map/ppermute | solution.py:371
  49.8 45.6 %collective-permute-start.3 = (bf16[512,512]{1,0:T(8,128)(2,1)S(1)}, bf16[512,512]{1,0:T(8,128)(2,1)S(1)}, u32[]{:S(2)}, u32[]{:S(2)}) collective-permute-start(bf16[512,512]{1,0:T(8,128)(2,1)S(1)} %bitcast.19), channel_id=1, source_target_pairs={{0,32},{32,0},{1,33},{33,1},{2,34},{34,2},{3,35},{35,3},{4,36},{36... | collective-permute-start | bytes 1572872 | tf_op jit(solution)/shard_map/ppermute | solution.py:383
  52.5 7.4 %copy-start = (s32[512]{0:T(512)S(1)}, s32[512]{0:T(512)}, u32[]{:S(2)}) copy-start(s32[512]{0:T(512)} %param.6) | copy-start | bytes 6148
  60.6 18.5 %all-to-all-start.2 = ((f32[8,4,512]{2,1,0:T(4,128)}), f32[8,4,512]{2,1,0:T(4,128)S(1)}, u32[]{:S(2)}, u32[]{:S(2)}) async-start(f32[8,4,512]{2,1,0:T(4,128)} %get-tuple-element.18.all_ref), calls=%async_computation.2 | async-start | bytes 131072 | tf_op jit(solution)/shard_map/all_to_all | solution.py:374
  64.0 31.4 %collective-permute-start.4 = (bf16[512,512]{1,0:T(8,128)(2,1)S(1)}, bf16[512,512]{1,0:T(8,128)(2,1)}, u32[]{:S(2)}, u32[]{:S(2)}) collective-permute-start(bf16[512,512]{1,0:T(8,128)(2,1)S(1)} %collective-permute-done.rest_1_), channel_id=1, source_target_pairs={{0,32},{32,0},{1,33},{33,1},{2,34},{34,2},{3,35},{35,3},{4,36},{36... | collective-permute-start | bytes 1572872 | tf_op jit(solution)/shard_map/ppermute | solution.py:383
  69.0 26.4 %collective-permute-start.5 = (bf16[512,512]{1,0:T(8,128)(2,1)S(1)}, bf16[512,512]{1,0:T(8,128)(2,1)}, u32[]{:S(2)}, u32[]{:S(2)}) collective-permute-start(bf16[512,512]{1,0:T(8,128)(2,1)S(1)} %collective-permute-done.1.rest_2_), channel_id=1, source_target_pairs={{0,32},{32,0},{1,33},{33,1},{2,34},{34,2},{3,35},{35,3},{4,36},{36... | collective-permute-start | bytes 1572872 | tf_op jit(solution)/shard_map/ppermute | solution.py:383
  72.0 23.4 %collective-permute-start.6 = (bf16[512,512]{1,0:T(8,128)(2,1)S(1)}, bf16[512,512]{1,0:T(8,128)(2,1)}, u32[]{:S(2)}, u32[]{:S(2)}) collective-permute-start(bf16[512,512]{1,0:T(8,128)(2,1)S(1)} %collective-permute-done.2.rest_3_), channel_id=1, source_target_pairs={{0,32},{32,0},{1,33},{33,1},{2,34},{34,2},{3,35},{35,3},{4,36},{36... | collective-permute-start | bytes 1572872 | tf_op jit(solution)/shard_map/ppermute | solution.py:383
  79.1 23.8 %all-to-all-start.3 = ((bf16[32,16,256]{2,1,0:T(8,128)(2,1)}), bf16[32,16,256]{2,1,0:T(8,128)(2,1)}, u32[]{:S(2)}, u32[]{:S(2)}) async-start(bf16[32,16,256]{2,1,0:T(8,128)(2,1)} %bitcast.2), calls=%async_computation.3 | async-start | bytes 524288 | tf_op jit(solution)/shard_map/all_to_all | solution.py:377

commit v2 on v1

--- a/solution.py
+++ b/solution.py
@@ -117,7 +117,7 @@
         mean_col[...] = as_cols(weighted / total)
 
 
-def local_stats(toks, rows, book, peers, cb=4096, sub=512):
+def local_stats(toks, rows, book, peers, cb=2048, sub=512):
     tokens, (codes, d) = toks.shape[0], book.shape
     steps = codes // cb
     cols = pl.BlockSpec((tokens, 128), lambda i: (0, 0))
@@ -206,7 +206,7 @@
     ]
 
 
-def lat_first(toks, m_col, mean_col, book, part=1, parts=2, cb=4096, sub=512):
+def lat_first(toks, m_col, mean_col, book, part=1, parts=2, cb=2048, sub=512):
     tokens, (codes, d) = toks.shape[0], book.shape
     steps = codes // cb * part // parts
     whole = pl.BlockSpec((tokens, d), lambda i: (0, 0))
@@ -222,7 +222,7 @@
     )(toks, toks, m_col, mean_col, book)
 
 
-def lat_second(toks, m_col, mean_col, book, a, b, rows, row, part=1, parts=2, cb=4096, sub=512):
+def lat_second(toks, m_col, mean_col, book, a, b, rows, row, part=1, parts=2, cb=2048, sub=512):
     tokens, (codes, d) = toks.shape[0], book.shape
     first = codes // cb * part // parts
     steps = codes // cb - first
@@ -242,9 +242,10 @@
     )(toks, toks, m_col, mean_col, book, a, b, rows, row)
 
 
-def combine_kernel(all_ref, tgt_ref, row_ref, loss_ref):
+def combine_kernel(all_ref, tgt_ref, first_ref, row_ref, loss_ref):
     stats = all_ref[...]
     m, l, w = stats[:, 0, :], stats[:, 1, :], stats[:, 2, :]
+    tokens = m.shape[1]
     top = jnp.max(m, axis=0, keepdims=True)
     scale = jnp.exp(m - top)
     total = jnp.sum(l * scale, axis=0, keepdims=True)
@@ -252,70 +253,74 @@
     lse = top + jnp.log(total)
     pack = jnp.concatenate([lse, mean, tgt_ref[...].astype(F32), mean], axis=0)
     row_ref[...] = jnp.broadcast_to(pack[None], row_ref.shape)
-    loss_ref[...] = lse - jnp.sum(stats[:, 3, :], axis=0, keepdims=True)
-
-
-def combine(stats, tgt, groups):
+    loss = jnp.broadcast_to(lse - jnp.sum(stats[:, 3, :], axis=0, keepdims=True), (8, tokens))
+    loss_ref[...] = pltpu.roll(loss, first_ref[0], 1)[:1, : loss_ref.shape[1]]
+
+
+def combine(stats, tgt, first, groups, count):
     tokens = stats.shape[-1]
+    vmem = pl.BlockSpec(memory_space=pltpu.VMEM)
     return pl.pallas_call(
         combine_kernel,
+        in_specs=[vmem, vmem, pl.BlockSpec(memory_space=pltpu.SMEM)],
         out_shape=[
             jax.ShapeDtypeStruct((groups, 4, tokens), F32),
-            jax.ShapeDtypeStruct((1, tokens), F32),
+            jax.ShapeDtypeStruct((1, count), F32),
         ],
         compiler_params=params(),
         cost_estimate=cost(tokens * 1000, tokens * 800),
         name="combine",
-    )(stats, tgt)
-
-
-def book_kernel(first, sub, s_ref, rows_ref, book_ref, *rest):
-    start, rest = (rest[:1], rest[1:]) if first else ((), rest)
+    )(stats, tgt, first)
+
+
+def book_kernel(sub, batch, s_ref, rows_ref, book_ref, *rest):
     groups = len(rest) - 3
     toks, (out_ref, buf, sem) = rest[:groups], rest[groups:]
     for g in range(groups):
         pltpu.make_async_copy(toks[g], buf.at[g], sem.at[g]).start()
     chunk, d = book_ref.shape
     tokens = buf.shape[1]
-    ids = lax.broadcasted_iota(jnp.int32, (sub, tokens), 0) + s_ref[s_ref.shape[0] - 1]
-    work = [(g, j) for g in range(groups) for j in range(chunk // sub)]
+    ids = lax.broadcasted_iota(jnp.int32, (sub, tokens), 0) + s_ref[groups]
+    out_ref[...] = jnp.zeros_like(out_ref)
 
     def block(j):
         return book_ref[j * sub : (j + 1) * sub, :]
 
-    def logits(g, j):
-        if j == 0:
-            pltpu.make_async_copy(toks[g], buf.at[g], sem.at[g]).wait()
-        return dot(block(j), buf[g, :, :d], NT)
-
-    ahead = logits(*work[0])
-    for n, (g, j) in enumerate(work):
-        logit = ahead
-        if n + 1 < len(work):
-            ahead = logits(*work[n + 1])
-        row = rows_ref[s_ref[first + g]]
-        back = dot(block(j), buf[g, :, d:], NT)
-        prob = jnp.exp(logit - row[0:1])
-        hit = jnp.where(ids + j * sub == row[2:3].astype(jnp.int32), 1.0, 0.0)
-        delta = prob * (back - row[1:2]) + ce_weight * (prob - hit)
-        out = dot(delta.astype(BF16), buf[g, :, :d], NN) + dot(hit.astype(BF16), buf[g, :, d:], NN)
-        at = slice(j * sub, (j + 1) * sub)
-        if g == 0 and not start:
-            out_ref[at, :] = out
-        else:
-            out_ref[at, :] = (start[0] if g == 0 else out_ref)[at, :] + out
-
-
-def book_grad(scalars, rows, book, toks, start=None, sub=512):
+    def step(i, carry):
+        work = [(i * batch + k, j) for k in range(batch) for j in range(chunk // sub)]
+
+        def logits(g, j):
+            if j == 0:
+                pltpu.make_async_copy(toks[0], buf.at[g], sem.at[g]).wait()
+            return dot(block(j), buf[g, :, :d], NT)
+
+        ahead = logits(*work[0])
+        for n, (g, j) in enumerate(work):
+            logit = ahead
+            if n + 1 < len(work):
+                ahead = logits(*work[n + 1])
+            row = rows_ref[s_ref[g]]
+            back = dot(block(j), buf[g, :, d:], NT)
+            prob = jnp.exp(logit - row[0:1])
+            hit = jnp.where(ids + j * sub == row[2:3].astype(jnp.int32), 1.0, 0.0)
+            delta = prob * (back - row[1:2]) + ce_weight * (prob - hit)
+            at = slice(j * sub, (j + 1) * sub)
+            out_ref[at, :] += dot(delta.astype(BF16), buf[g, :, :d], NN) + dot(
+                hit.astype(BF16), buf[g, :, d:], NN
+            )
+        return carry
+
+    lax.fori_loop(0, groups // batch, step, 0)
+
+
+def book_grad(scalars, rows, book, toks, sub=512, batch=1):
     groups = len(toks)
     (tokens, width), (chunk, d) = toks[0].shape, book.shape
     whole = pl.BlockSpec((chunk, d), lambda i, s: (0, 0))
-    extra = [] if start is None else [start]
     grid_spec = pltpu.PrefetchScalarGridSpec(
         num_scalar_prefetch=1,
         grid=(1,),
         in_specs=[pl.BlockSpec(rows.shape, lambda i, s: (0, 0, 0)), whole]
-        + [whole for _ in extra]
         + [pl.BlockSpec(memory_space=pl.ANY)] * groups,
         out_specs=whole,
         scratch_shapes=[
@@ -324,15 +329,43 @@
         ],
     )
     return pl.pallas_call(
-        functools.partial(book_kernel, 0 if start is None else groups, sub),
+        functools.partial(book_kernel, sub, batch),
         grid_spec=grid_spec,
         out_shape=jax.ShapeDtypeStruct((chunk, d), F32),
         compiler_params=params(),
         cost_estimate=cost(
             8 * groups * tokens * chunk * d, groups * tokens * width * 2, groups * tokens * chunk
         ),
-        name="book_first" if start is None else "book_second",
-    )(scalars, rows, book, *extra, *toks)
+        name="book_grad",
+    )(scalars, rows, book, *toks)
+
+
+def spread_kernel(lat_ref, grad_ref, out_ref):
+    both = jnp.concatenate([lat_ref[...], grad_ref[...]], axis=1)
+    out_ref[...] = jnp.broadcast_to(both[None], out_ref.shape)
+
+
+def spread(lat, grad, peers):
+    count, d = lat.shape
+    return pl.pallas_call(
+        spread_kernel,
+        out_shape=jax.ShapeDtypeStruct((peers, count, 2 * d), BF16),
+        compiler_params=params(),
+        name="spread",
+    )(lat, grad)
+
+
+def gather_kernel(in_ref, out_ref):
+    out_ref[...] = jnp.sum(in_ref[...].astype(F32), axis=0).astype(out_ref.dtype)
+
+
+def sum_parts(parts):
+    return pl.pallas_call(
+        gather_kernel,
+        out_shape=jax.ShapeDtypeStruct(parts.shape[1:], BF16),
+        compiler_params=params(),
+        name="sum_parts",
+    )(parts)
 
 
 def in_hbm(*arrays):
@@ -351,8 +384,7 @@
     swap = [(0, 1), (1, 0)]
     book = pltpu.with_memory_space_constraint(codebook, pltpu.HBM)
 
-    both = jnp.concatenate([latents, out_grad], axis=1)
-    toks = lax.all_to_all(jnp.broadcast_to(both[None], (peers, own_count, 2 * d)), ZY, 0, 0)
+    toks = lax.all_to_all(spread(*in_hbm(latents, out_grad), peers), ZY, 0, 0)
     toks = toks.reshape(tokens, 2 * d)
     local_ids = targets - code_pos * code_dev
     rows = pick_rows(jnp.broadcast_to(local_ids[:, None], (tokens, 128)), book)
@@ -365,24 +397,23 @@
     packed, m_col, mean_col = local_stats(toks, rows, book, peers)
     m_col, mean_col = in_hbm(m_col, mean_col)
     stats = lax.all_to_all(packed, ZY, 0, 0)
-    late = lax.optimization_barrier((toks, packed))[0]
-    same = [late]
+    same = [toks]
     for k in range(1, nx):
-        same.append(lax.ppermute(late, "x", [(i, (i + k) % nx) for i in range(nx)]))
+        same.append(lax.ppermute(toks, "x", [(i, (i + k) % nx) for i in range(nx)]))
     a, b = lat_first(toks, m_col, mean_col, book)
-    row, loss = combine(stats, targets[None], 2 * nx)
+    shift = lax.rem(tokens - code_pos * own_count, tokens).astype(jnp.int32).reshape(1)
+    row, loss = combine(stats, targets[None], shift, 2 * nx, own_count)
     everyone = lax.all_to_all(row, XC, 0, 0)
     part = lat_second(toks, m_col, mean_col, book, *in_hbm(a, b), rows, row)
     part, everyone = lax.optimization_barrier((part, everyone))
     moved = lax.all_to_all(part.reshape(peers, own_count, d), ZY, 0, 0)
-    latent_grad = jnp.sum(moved.astype(F32), axis=0).astype(BF16)
-    token_loss = lax.dynamic_slice(loss, (0, code_pos * own_count), (1, own_count)).reshape(own_count)
+    latent_grad = sum_parts(moved)
+    token_loss = loss.reshape(own_count)
 
     other = []
     for piece in same:
         other.append(lax.ppermute(piece, "core", swap))
-    half = book_grad(scalars, everyone, own_book, same)
-    codebook_grad = book_grad(scalars, everyone, own_book, other, half)
+    codebook_grad = book_grad(scalars, everyone, own_book, same + other)
     return latent_grad, codebook_grad, token_loss
 
 

time: 105 us -> 97.8 us (0.931)
  starting transfers between devices: 41.1 us -> 37.5 us
  waiting for transfers between devices: 14.4 us -> 11.8 us
  Pallas kernels: 42.5 us -> 45 us
  other arithmetic: 3.01 us -> 0.69 us
  local copies, waits for them, and re-layouts: 2.72 us -> 1.3 us
    all_to_all x1, starting transfers between devices: 9.57 us -> 5.25 us  [per_device(): moved = lax.all_to_all(part.reshape(peers, own_count, d), ZY, 0, 0)]
    ppermute x3, waiting for transfers between devices: 4.71 us -> 2.13 us  [per_device(): same.append(lax.ppermute(toks, 'x', [(i, (i + k) % nx) for i in range(nx)]))]
    pallas_call x3 -> x4, Pallas kernels: 14.9 us -> 16.8 us  [the longest x1 13.8 us: book_grad(): pl.pallas_call(functools.partial(book_kernel, sub, batch), grid_spec=grid...]
    reduce_sum x1 -> x0, other arithmetic: 1.61 us -> none  [per_device(): latent_grad = jnp.sum(moved.astype(F32), axis=0).astype(BF16)]
  transfers between devices with their start and end apart: 11 -> 11, of which waited for: 2 -> 2; matrix products, arithmetic and copies ran while one was open for 2% -> 2% of each run, Pallas kernels for 33% -> 44%
where the time goes in v2:
time: 97.8 us; the launch traced here: 97.1 us
  Pallas kernels  45 us (46%)
  starting transfers between devices  37.5 us (38%)
  waiting for transfers between devices  11.8 us (12%)
  local copies, waits for them, and re-layouts  1.3 us (1%)
    pallas_call x1, Pallas kernels, book_grad(): pl.pallas_call(functools.partial(book_kernel, sub, batch), grid_spec=grid...  13.8 us
    all_to_all x1, starting transfers between devices, per_device(): toks = lax.all_to_all(spread(*in_hbm(latents, out_grad), peers), ZY, 0, 0)  12 us
    all_to_all x1, waiting for transfers between devices, per_device(): toks = lax.all_to_all(spread(*in_hbm(latents, out_grad), peers), ZY, 0, 0)  9.68 us
    pallas_call x1, Pallas kernels, local_stats(): pl.pallas_call(functools.partial(stats_kernel, steps, sub), grid=(steps,)...  8.34 us
    pallas_call x1, Pallas kernels, lat_first(): pl.pallas_call(functools.partial(first_kernel, sub), grid=(steps,), in_sp...  7.26 us
    pallas_call x1, Pallas kernels, lat_second(): pl.pallas_call(functools.partial(second_kernel, steps, sub), grid=(steps,...  6.91 us
    ppermute x4, starting transfers between devices, per_device(): other.append(lax.ppermute(piece, 'core', swap))  6.14 us
    pallas_call x1, Pallas kernels, pick_rows(): pl.pallas_call(functools.partial(pick_kernel, cb), grid=(codes // cb,), i...  5.67 us
  transfers between devices with their start and end apart: 11, of which 2 were waited for; matrix products, arithmetic and copies ran while one was open for 2% of the time, Pallas kernels for 44%

profile of v2, /device:TPU:1, one launch (start us, length us, event | category | flops | bytes accessed | tf_op | source)
XLA Modules:
  0.0 97.1 jit_solution(7862543610867043900)
XLA Ops:
  0.6 1.6 %spread.1 = bf16[32,16,512]{2,1,0:T(8,128)(2,1)} custom-call(bf16[16,256]{1,0:T(8,128)(2,1)} %lat_ref.1, bf16[16,256]{1,0:T(8,128)(2,1)} %grad_ref.1), custom_call_target="tpu_custom_call" | custom-call | tf_op jit(solution)/shard_map/spread/pallas_call | solution.py:350
  2.2 12.0 %all-to-all-start = ((bf16[32,16,512]{2,1,0:T(8,128)(2,1)}), bf16[32,16,512]{2,1,0:T(8,128)(2,1)S(1)}, u32[]{:S(2)}, u32[]{:S(2)}) async-start(bf16[32,16,512]{2,1,0:T(8,128)(2,1)} %spread.1), calls=%async_computation | async-start | bytes 1048576 | tf_op jit(solution)/shard_map/all_to_all | solution.py:387
  14.3 0.1 stack.39.s_ref
  14.3 0.7 broadcast_subtract_fusion
  15.0 0.1 broadcast_in_dim.4.tgt_ref
  15.2 5.7 %pick.1.rows_ref = f32[512,256]{1,0:T(8,128)} custom-call(s32[512,128]{1,0:T(8,128)S(1)} %broadcast_in_dim.4.tgt_ref, bf16[8192,256]{1,0:T(8,128)(2,1)} %book_ref.7), custom_call_target="tpu_custom_call" | custom-call | flops 2147483648 | bytes 4194304 | tf_op jit(solution)/shard_map/pick/pallas_call | solution.py:49
  20.8 9.7 %all-to-all-done = bf16[32,16,512]{2,1,0:T(8,128)(2,1)S(1)} async-done(((bf16[32,16,512]{2,1,0:T(8,128)(2,1)}), bf16[32,16,512]{2,1,0:T(8,128)(2,1)S(1)}, u32[]{:S(2)}, u32[]{:S(2)}) %all-to-all-start) | async-done | bytes 524320 | tf_op jit(solution)/shard_map/all_to_all | solution.py:387
  30.5 1.2 %collective-permute-start = (bf16[512,512]{1,0:T(8,128)(2,1)S(1)}, bf16[512,512]{1,0:T(8,128)(2,1)S(1)}, u32[]{:S(2)}, u32[]{:S(2)}) collective-permute-start(bf16[512,512]{1,0:T(8,128)(2,1)S(1)} %bitcast.14), channel_id=1, source_target_pairs={{0,64},{64,128},{128,192},{192,0},{1,65},{65,129},{129,193},{193,1... | collective-permute-start | bytes 1572872 | tf_op jit(solution)/shard_map/ppermute | solution.py:402
  31.7 2.5 %collective-permute-start.1 = (bf16[512,512]{1,0:T(8,128)(2,1)S(1)}, bf16[512,512]{1,0:T(8,128)(2,1)S(1)}, u32[]{:S(2)}, u32[]{:S(2)}) collective-permute-start(bf16[512,512]{1,0:T(8,128)(2,1)S(1)} %bitcast.15), channel_id=1, source_target_pairs={{0,128},{64,192},{128,0},{192,64},{1,129},{65,193},{129,1},{193,65... | collective-permute-start | bytes 1572872 | tf_op jit(solution)/shard_map/ppermute | solution.py:402
  34.2 1.2 %collective-permute-start.2 = (bf16[512,512]{1,0:T(8,128)(2,1)S(1)}, bf16[512,512]{1,0:T(8,128)(2,1)S(1)}, u32[]{:S(2)}, u32[]{:S(2)}) collective-permute-start(bf16[512,512]{1,0:T(8,128)(2,1)S(1)} %bitcast.16), channel_id=1, source_target_pairs={{0,192},{64,0},{128,64},{192,128},{1,193},{65,1},{129,65},{193,129... | collective-permute-start | bytes 1572872 | tf_op jit(solution)/shard_map/ppermute | solution.py:402
  35.3 8.3 %stats.1 = (f32[32,4,512]{2,1,0:T(4,128)}, f32[512,128]{1,0:T(8,128)}, f32[512,128]{1,0:T(8,128)}) custom-call(bf16[512,512]{1,0:T(8,128)(2,1)S(1)} %bitcast.17, bf16[512,512]{1,0:T(8,128)(2,1)S(1)} %bitcast.18, f32[512,256]{1,0:T(8,128)} %pick.1.rows_ref, bf16[8192,256]{1,0:T(8,128)(2,1)} %book_ref.7), custom_call_target="tpu_custom_call" | custom-call | flops 4294967296 | bytes 4194304 | tf_op jit(solution)/shard_map/stats/pallas_call | solution.py:124
  43.7 5.3 %all-to-all-start.1 = ((f32[32,4,512]{2,1,0:T(4,128)}), f32[32,4,512]{2,1,0:T(4,128)S(1)}, u32[]{:S(2)}, u32[]{:S(2)}) async-start(f32[32,4,512]{2,1,0:T(4,128)} %get-tuple-element.16), calls=%async_computation.1 | async-start | bytes 524288 | tf_op jit(solution)/shard_map/all_to_all | solution.py:399
  48.9 1.1 %constant_dynamic-slice_fusion.book_ref = bf16[1024,256]{1,0:T(8,128)(2,1)S(1)} fusion(bf16[8192,256]{1,0:T(8,128)(2,1)} %book_ref.7, s32[]{:T(128)S(6)} %select_n.3), kind=kLoop, calls=%fused_computation.1 | loop fusion | bytes 1048580 | tf_op jit(solution)/shard_map/dynamic_slice | solution.py:396
  50.0 2.7 %collective-permute-start.3 = (bf16[512,512]{1,0:T(8,128)(2,1)S(1)}, bf16[512,512]{1,0:T(8,128)(2,1)S(1)}, u32[]{:S(2)}, u32[]{:S(2)}) collective-permute-start(bf16[512,512]{1,0:T(8,128)(2,1)S(1)} %bitcast.19), channel_id=1, source_target_pairs={{0,32},{32,0},{1,33},{33,1},{2,34},{34,2},{3,35},{35,3},{4,36},{36... | collective-permute-start | bytes 1572872 | tf_op jit(solution)/shard_map/ppermute | solution.py:415
  52.8 0.1 collective-permute-start.4
  52.9 2.1 %collective-permute-done.1.rest_2_ = bf16[512,512]{1,0:T(8,128)(2,1)S(1)} collective-permute-done((bf16[512,512]{1,0:T(8,128)(2,1)S(1)}, bf16[512,512]{1,0:T(8,128)(2,1)S(1)}, u32[]{:S(2)}, u32[]{:S(2)}) %collective-permute-start.1) | collective-permute-done | bytes 524320 | tf_op jit(solution)/shard_map/ppermute | solution.py:402
  55.0 3.3 %collective-permute-start.5 = (bf16[512,512]{1,0:T(8,128)(2,1)S(1)}, bf16[512,512]{1,0:T(8,128)(2,1)}, u32[]{:S(2)}, u32[]{:S(2)}) collective-permute-start(bf16[512,512]{1,0:T(8,128)(2,1)S(1)} %collective-permute-done.1.rest_2_), channel_id=1, source_target_pairs={{0,32},{32,0},{1,33},{33,1},{2,34},{34,2},{3,35},{35,3},{4,36},{36... | collective-permute-start | bytes 1572872 | tf_op jit(solution)/shard_map/ppermute | solution.py:415
  58.3 7.3 %lat_first.1 = (f32[512,256]{1,0:T(8,128)}, f32[512,256]{1,0:T(8,128)}) custom-call(bf16[512,512]{1,0:T(8,128)(2,1)S(1)} %bitcast.20, bf16[512,512]{1,0:T(8,128)(2,1)S(1)} %bitcast.21, f32[512,128]{1,0:T(8,128)} %get-tuple-element.12.m_ref, f32[512,128]{1,0:T(8,128)} %get-tuple-element.13.mean_ref, bf16[8192,256]{1,0:T(8,128)(2,1)} %book_ref.7), custom_call_target="tpu_custom_call" | custom-call | flops 4294967296 | bytes 2097152 | tf_op jit(solution)/shard_map/lat_first/pallas_call | solution.py:213
  65.6 0.8 combine.1
  66.3 4.0 %all-to-all-start.2 = ((f32[8,4,512]{2,1,0:T(4,128)}), f32[8,4,512]{2,1,0:T(4,128)S(1)}, u32[]{:S(2)}, u32[]{:S(2)}) async-start(f32[8,4,512]{2,1,0:T(4,128)} %get-tuple-element.17.all_ref), calls=%async_computation.2 | async-start | bytes 131072 | tf_op jit(solution)/shard_map/all_to_all | solution.py:406
  70.4 6.9 %lat_second.1 = bf16[512,256]{1,0:T(8,128)(2,1)} custom-call(bf16[512,512]{1,0:T(8,128)(2,1)S(1)} %bitcast.22, bf16[512,512]{1,0:T(8,128)(2,1)S(1)} %bitcast.23, f32[512,128]{1,0:T(8,128)} %get-tuple-element.12.m_ref, f32[512,128]{1,0:T(8,128)} %get-tuple-element.13.mean_ref, bf16[8192,256]{1,0:T(8,128)(2,1)} %book_ref.7, f32[512,256]{1,0:T(8,128)} %get-tuple-element.14.a0, ...), custom_call_target="tpu_custom_call" | custom-call | flops 3221225472 | bytes 2097152 | tf_op jit(solution)/shard_map/lat_second/pallas_call | solution.py:230
  77.3 5.3 %all-to-all-start.3 = ((bf16[32,16,256]{2,1,0:T(8,128)(2,1)}), bf16[32,16,256]{2,1,0:T(8,128)(2,1)S(1)}, u32[]{:S(2)}, u32[]{:S(2)}) async-start(bf16[32,16,256]{2,1,0:T(8,128)(2,1)} %bitcast.3), calls=%async_computation.3 | async-start | bytes 524288 | tf_op jit(solution)/shard_map/all_to_all | solution.py:409
  82.6 13.8 %book_grad.1 = f32[1024,256]{1,0:T(8,128)} custom-call(s32[9]{0:T(128)S(1)} %stack.39.s_ref, f32[8,4,512]{2,1,0:T(4,128)S(1)} %all-to-all-done.2.rows_ref, bf16[1024,256]{1,0:T(8,128)(2,1)S(1)} %constant_dynamic-slice_fusion.book_ref, bf16[512,512]{1,0:T(8,128)(2,1)S(1)} %bitcast.24, bf16[512,512]{1,0:T(8,128)(2,1)S(1)} %collective-permute-done.rest_1_, ...), custom_call_target="tpu_custom_call" | custom-call | flops 8589934592 | bytes 4194304 | tf_op jit(solution)/shard_map/book_grad/pallas_call | solution.py:331
  96.4 0.6 sum_parts.1
  (12 shorter events, 0.0 us)
Async XLA Ops:
  2.2 28.3 %all-to-all-start = ((bf16[32,16,512]{2,1,0:T(8,128)(2,1)}), bf16[32,16,512]{2,1,0:T(8,128)(2,1)S(1)}, u32[]{:S(2)}, u32[]{:S(2)}) async-start(bf16[32,16,512]{2,1,0:T(8,128)(2,1)} %spread.1), calls=%async_computation | async-start | bytes 1048576 | tf_op jit(solution)/shard_map/all_to_all | solution.py:387
  30.5 22.2 %collective-permute-start = (bf16[512,512]{1,0:T(8,128)(2,1)S(1)}, bf16[512,512]{1,0:T(8,128)(2,1)S(1)}, u32[]{:S(2)}, u32[]{:S(2)}) collective-permute-start(bf16[512,512]{1,0:T(8,128)(2,1)S(1)} %bitcast.14), channel_id=1, source_target_pairs={{0,64},{64,128},{128,192},{192,0},{1,65},{65,129},{129,193},{193,1... | collective-permute-start | bytes 1572872 | tf_op jit(solution)/shard_map/ppermute | solution.py:402
  31.7 23.3 %collective-permute-start.1 = (bf16[512,512]{1,0:T(8,128)(2,1)S(1)}, bf16[512,512]{1,0:T(8,128)(2,1)S(1)}, u32[]{:S(2)}, u32[]{:S(2)}) collective-permute-start(bf16[512,512]{1,0:T(8,128)(2,1)S(1)} %bitcast.15), channel_id=1, source_target_pairs={{0,128},{64,192},{128,0},{192,64},{1,129},{65,193},{129,1},{193,65... | collective-permute-start | bytes 1572872 | tf_op jit(solution)/shard_map/ppermute | solution.py:402
  34.2 24.1 %collective-permute-start.2 = (bf16[512,512]{1,0:T(8,128)(2,1)S(1)}, bf16[512,512]{1,0:T(8,128)(2,1)S(1)}, u32[]{:S(2)}, u32[]{:S(2)}) collective-permute-start(bf16[512,512]{1,0:T(8,128)(2,1)S(1)} %bitcast.16), channel_id=1, source_target_pairs={{0,192},{64,0},{128,64},{192,128},{1,193},{65,1},{129,65},{193,129... | collective-permute-start | bytes 1572872 | tf_op jit(solution)/shard_map/ppermute | solution.py:402
  43.7 21.9 %all-to-all-start.1 = ((f32[32,4,512]{2,1,0:T(4,128)}), f32[32,4,512]{2,1,0:T(4,128)S(1)}, u32[]{:S(2)}, u32[]{:S(2)}) async-start(f32[32,4,512]{2,1,0:T(4,128)} %get-tuple-element.16), calls=%async_computation.1 | async-start | bytes 524288 | tf_op jit(solution)/shard_map/all_to_all | solution.py:399
  50.0 32.5 %collective-permute-start.3 = (bf16[512,512]{1,0:T(8,128)(2,1)S(1)}, bf16[512,512]{1,0:T(8,128)(2,1)S(1)}, u32[]{:S(2)}, u32[]{:S(2)}) collective-permute-start(bf16[512,512]{1,0:T(8,128)(2,1)S(1)} %bitcast.19), channel_id=1, source_target_pairs={{0,32},{32,0},{1,33},{33,1},{2,34},{34,2},{3,35},{35,3},{4,36},{36... | collective-permute-start | bytes 1572872 | tf_op jit(solution)/shard_map/ppermute | solution.py:415
  52.8 29.8 %collective-permute-start.4 = (bf16[512,512]{1,0:T(8,128)(2,1)S(1)}, bf16[512,512]{1,0:T(8,128)(2,1)}, u32[]{:S(2)}, u32[]{:S(2)}) collective-permute-start(bf16[512,512]{1,0:T(8,128)(2,1)S(1)} %collective-permute-done.rest_1_), channel_id=1, source_target_pairs={{0,32},{32,0},{1,33},{33,1},{2,34},{34,2},{3,35},{35,3},{4,36},{36... | collective-permute-start | bytes 1572872 | tf_op jit(solution)/shard_map/ppermute | solution.py:415
  55.0 27.6 %collective-permute-start.5 = (bf16[512,512]{1,0:T(8,128)(2,1)S(1)}, bf16[512,512]{1,0:T(8,128)(2,1)}, u32[]{:S(2)}, u32[]{:S(2)}) collective-permute-start(bf16[512,512]{1,0:T(8,128)(2,1)S(1)} %collective-permute-done.1.rest_2_), channel_id=1, source_target_pairs={{0,32},{32,0},{1,33},{33,1},{2,34},{34,2},{3,35},{35,3},{4,36},{36... | collective-permute-start | bytes 1572872 | tf_op jit(solution)/shard_map/ppermute | solution.py:415
  58.3 24.3 %collective-permute-start.6 = (bf16[512,512]{1,0:T(8,128)(2,1)S(1)}, bf16[512,512]{1,0:T(8,128)(2,1)}, u32[]{:S(2)}, u32[]{:S(2)}) collective-permute-start(bf16[512,512]{1,0:T(8,128)(2,1)S(1)} %collective-permute-done.2.rest_3_), channel_id=1, source_target_pairs={{0,32},{32,0},{1,33},{33,1},{2,34},{34,2},{3,35},{35,3},{4,36},{36... | collective-permute-start | bytes 1572872 | tf_op jit(solution)/shard_map/ppermute | solution.py:415
  58.3 7.3 %copy-start = (s32[512]{0:T(512)S(1)}, s32[512]{0:T(512)}, u32[]{:S(2)}) copy-start(s32[512]{0:T(512)} %param.6) | copy-start | bytes 6148
  66.3 11.0 %all-to-all-start.2 = ((f32[8,4,512]{2,1,0:T(4,128)}), f32[8,4,512]{2,1,0:T(4,128)S(1)}, u32[]{:S(2)}, u32[]{:S(2)}) async-start(f32[8,4,512]{2,1,0:T(4,128)} %get-tuple-element.17.all_ref), calls=%async_computation.2 | async-start | bytes 131072 | tf_op jit(solution)/shard_map/all_to_all | solution.py:406
  77.3 19.2 %all-to-all-start.3 = ((bf16[32,16,256]{2,1,0:T(8,128)(2,1)}), bf16[32,16,256]{2,1,0:T(8,128)(2,1)S(1)}, u32[]{:S(2)}, u32[]{:S(2)}) async-start(bf16[32,16,256]{2,1,0:T(8,128)(2,1)} %bitcast.3), calls=%async_computation.3 | async-start | bytes 524288 | tf_op jit(solution)/shard_map/all_to_all | solution.py:409

commit v3 on v2

--- a/solution.py
+++ b/solution.py
@@ -73,11 +73,15 @@
     return jnp.broadcast_to(row, (128, row.shape[1])).T
 
 
-def stats_kernel(steps, sub, lat_ref, grad_ref, rows_ref, book_ref, out_ref, m_col, mean_col, m_s, l_s, w_s):
+def stats_kernel(
+    steps, sub, lat_ref, grad_ref, book_ref, rows_hbm, out_ref, m_col, mean_col, m_s, l_s, w_s, rows_ref, sem
+):
     i = pl.program_id(0)
+    load = pltpu.make_async_copy(rows_hbm, rows_ref, sem)
 
     @pl.when(i == 0)
     def _():
+        load.start()
         m_s[...] = jnp.full_like(m_s, -jnp.inf)
         l_s[...] = jnp.zeros_like(l_s)
         w_s[...] = jnp.zeros_like(w_s)
@@ -110,6 +114,7 @@
         scale = jnp.exp(m - top)
         total = jnp.sum(l_s[...] * scale, axis=0, keepdims=True)
         weighted = jnp.sum(w_s[...] * scale, axis=0, keepdims=True)
+        load.wait()
         picked = as_row(fold(lat_ref[...].astype(F32) * rows_ref[...]))
         pack = jnp.concatenate([top, total, weighted, picked], axis=0)
         out_ref[...] = jnp.broadcast_to(pack[None], out_ref.shape)
@@ -127,8 +132,8 @@
         in_specs=[
             pl.BlockSpec((tokens, d), lambda i: (0, 0)),
             pl.BlockSpec((tokens, d), lambda i: (0, 1)),
-            pl.BlockSpec((tokens, d), lambda i: (0, 0)),
             pl.BlockSpec((cb, d), lambda i: (i, 0)),
+            pl.BlockSpec(memory_space=pltpu.HBM),
         ],
         out_specs=[pl.BlockSpec((peers, 4, tokens), lambda i: (0, 0, 0)), cols, cols],
         out_shape=[
@@ -136,11 +141,12 @@
             pltpu.HBM((tokens, 128), F32),
             pltpu.HBM((tokens, 128), F32),
         ],
-        scratch_shapes=[pltpu.VMEM((8, tokens), F32)] * 3,
+        scratch_shapes=[pltpu.VMEM((8, tokens), F32)] * 3
+        + [pltpu.VMEM((tokens, d), F32), pltpu.SemaphoreType.DMA],
         compiler_params=params(),
         cost_estimate=cost(4 * tokens * codes * d, codes * d * 2, tokens * codes),
         name="stats",
-    )(toks, toks, rows, book)
+    )(toks, toks, book, rows)
 
 
 def lat_step(sub, lat_ref, grad_ref, m_ref, book_ref, outs, weigh):
@@ -175,25 +181,34 @@
 
 
 def second_kernel(
-    steps, sub, lat_ref, grad_ref, m_ref, mean_ref, book_ref, a0, b0, rows_ref, all_ref,
-    part_ref, sum_ref, lse_col, mean_col,
+    steps, sub, lat_ref, grad_ref, book_ref, all_ref, m_hbm, mean_hbm, a_hbm, b_hbm, rows_hbm,
+    part_ref, sum_ref, lse_col, mean_col, m_ref, own_mean, a_ref, b_ref, rows_ref, sem,
 ):
-    @pl.when(pl.program_id(0) == 0)
-    def _():
+    i = pl.program_id(0)
+    pairs = ((m_hbm, m_ref), (mean_hbm, own_mean), (a_hbm, a_ref), (b_hbm, b_ref), (rows_hbm, rows_ref))
+    loads = [pltpu.make_async_copy(src, dst, sem.at[n]) for n, (src, dst) in enumerate(pairs)]
+
+    @pl.when(i == 0)
+    def _():
+        for load in loads:
+            load.start()
         lse_col[...] = as_cols(all_ref[0, 0:1, :])
         mean_col[...] = as_cols(all_ref[0, 1:2, :])
-        own = jnp.exp(m_ref[...] - lse_col[...])
-        ratio = own * (ce_weight + mean_ref[...] - mean_col[...])
-        sum_ref[...] = own[:, :1] * a0[...] + ratio[:, :1] * b0[...] - ce_weight * rows_ref[...]
+        sum_ref[...] = jnp.zeros_like(sum_ref)
 
     def weigh(prob, back):
         return (prob * (back - mean_col[:, :1]) + ce_weight * prob,)
 
     lat_step(sub, lat_ref, grad_ref, lse_col, book_ref, (sum_ref,), weigh)
 
-    @pl.when(pl.program_id(0) == steps - 1)
-    def _():
-        part_ref[...] = sum_ref[...].astype(part_ref.dtype)
+    @pl.when(i == steps - 1)
+    def _():
+        for load in loads:
+            load.wait()
+        own = jnp.exp(m_ref[...] - lse_col[...])
+        ratio = own * (ce_weight + own_mean[...] - mean_col[...])
+        part = own[:, :1] * a_ref[...] + ratio[:, :1] * b_ref[...] - ce_weight * rows_ref[...]
+        part_ref[...] = (sum_ref[...] + part).astype(part_ref.dtype)
 
 
 def lat_specs(tokens, d, cb, first):
@@ -230,16 +245,23 @@
     return pl.pallas_call(
         functools.partial(second_kernel, steps, sub),
         grid=(steps,),
-        in_specs=lat_specs(tokens, d, cb, first)
-        + [whole] * 3
-        + [pl.BlockSpec((1, 4, tokens), lambda i: (0, 0, 0))],
+        in_specs=[
+            pl.BlockSpec((tokens, d), lambda i: (0, 0)),
+            pl.BlockSpec((tokens, d), lambda i: (0, 1)),
+            pl.BlockSpec((cb, d), lambda i: (i + first, 0)),
+            pl.BlockSpec((1, 4, tokens), lambda i: (0, 0, 0)),
+        ]
+        + [pl.BlockSpec(memory_space=pltpu.HBM)] * 5,
         out_specs=whole,
         out_shape=jax.ShapeDtypeStruct((tokens, d), BF16),
-        scratch_shapes=[pltpu.VMEM((tokens, d), F32)] + [pltpu.VMEM((tokens, 128), F32)] * 2,
+        scratch_shapes=[pltpu.VMEM((tokens, d), F32)]
+        + [pltpu.VMEM((tokens, 128), F32)] * 4
+        + [pltpu.VMEM((tokens, d), F32)] * 3
+        + [pltpu.SemaphoreType.DMA((5,))],
         compiler_params=params(),
         cost_estimate=cost(6 * tokens * cb * steps * d, cb * steps * d * 2, tokens * cb * steps),
         name="lat_second",
-    )(toks, toks, m_col, mean_col, book, a, b, rows, row)
+    )(toks, toks, book, row, m_col, mean_col, a, b, rows)
 
 
 def combine_kernel(all_ref, tgt_ref, first_ref, row_ref, loss_ref):
@@ -313,7 +335,7 @@
     lax.fori_loop(0, groups // batch, step, 0)
 
 
-def book_grad(scalars, rows, book, toks, sub=512, batch=1):
+def book_grad(scalars, rows, book, toks, sub=1024, batch=1):
     groups = len(toks)
     (tokens, width), (chunk, d) = toks[0].shape, book.shape
     whole = pl.BlockSpec((chunk, d), lambda i, s: (0, 0))

time: 97.8 us -> 96.9 us (level)
  Pallas kernels: 45 us -> 44 us
  transfers between devices with their start and end apart: 11 -> 11, of which waited for: 2 -> 2; matrix products, arithmetic and copies ran while one was open for 2% -> 2% of each run, Pallas kernels for 44% -> 43%
where the time goes in v3:
time: 96.9 us; the launch traced here: 96.2 us
  Pallas kernels  44 us (45%)
  starting transfers between devices  37.5 us (39%)
  waiting for transfers between devices  11.9 us (12%)
  local copies, waits for them, and re-layouts  1.3 us (1%)
    pallas_call x1, Pallas kernels, book_grad(): pl.pallas_call(functools.partial(book_kernel, sub, batch), grid_spec=grid...  13.4 us
    all_to_all x1, starting transfers between devices, per_device(): toks = lax.all_to_all(spread(*in_hbm(latents, out_grad), peers), ZY, 0, 0)  12 us
    all_to_all x1, waiting for transfers between devices, per_device(): toks = lax.all_to_all(spread(*in_hbm(latents, out_grad), peers), ZY, 0, 0)  9.68 us
    pallas_call x1, Pallas kernels, local_stats(): pl.pallas_call(functools.partial(stats_kernel, steps, sub), grid=(steps,)...  8.24 us
    pallas_call x1, Pallas kernels, lat_first(): pl.pallas_call(functools.partial(first_kernel, sub), grid=(steps,), in_sp...  7.26 us
    pallas_call x1, Pallas kernels, lat_second(): pl.pallas_call(functools.partial(second_kernel, steps, sub), grid=(steps,...  6.42 us
    ppermute x4, starting transfers between devices, per_device(): other.append(lax.ppermute(piece, 'core', swap))  6.14 us
    pallas_call x1, Pallas kernels, pick_rows(): pl.pallas_call(functools.partial(pick_kernel, cb), grid=(codes // cb,), i...  5.67 us
  transfers between devices with their start and end apart: 11, of which 2 were waited for; matrix products, arithmetic and copies ran while one was open for 2% of the time, Pallas kernels for 43%

profile of v3, /device:TPU:1, one launch (start us, length us, event | category | flops | bytes accessed | tf_op | source)
XLA Modules:
  0.0 96.2 jit_solution(7292135674810403573)
XLA Ops:
  0.6 1.6 %spread.1 = bf16[32,16,512]{2,1,0:T(8,128)(2,1)} custom-call(bf16[16,256]{1,0:T(8,128)(2,1)} %lat_ref.1, bf16[16,256]{1,0:T(8,128)(2,1)} %grad_ref.1), custom_call_target="tpu_custom_call" | custom-call | tf_op jit(solution)/shard_map/spread/pallas_call | solution.py:372
  2.2 12.0 %all-to-all-start = ((bf16[32,16,512]{2,1,0:T(8,128)(2,1)}), bf16[32,16,512]{2,1,0:T(8,128)(2,1)S(1)}, u32[]{:S(2)}, u32[]{:S(2)}) async-start(bf16[32,16,512]{2,1,0:T(8,128)(2,1)} %spread.1), calls=%async_computation | async-start | bytes 1048576 | tf_op jit(solution)/shard_map/all_to_all | solution.py:409
  14.3 0.1 stack.39.s_ref
  14.3 0.7 broadcast_subtract_fusion
  15.0 0.1 broadcast_in_dim.4.tgt_ref
  15.2 5.7 %pick.1.rows_hbm = f32[512,256]{1,0:T(8,128)} custom-call(s32[512,128]{1,0:T(8,128)S(1)} %broadcast_in_dim.4.tgt_ref, bf16[8192,256]{1,0:T(8,128)(2,1)} %book_ref.7), custom_call_target="tpu_custom_call" | custom-call | flops 2147483648 | bytes 4194304 | tf_op jit(solution)/shard_map/pick/pallas_call | solution.py:49
  20.8 9.7 %all-to-all-done = bf16[32,16,512]{2,1,0:T(8,128)(2,1)S(1)} async-done(((bf16[32,16,512]{2,1,0:T(8,128)(2,1)}), bf16[32,16,512]{2,1,0:T(8,128)(2,1)S(1)}, u32[]{:S(2)}, u32[]{:S(2)}) %all-to-all-start) | async-done | bytes 524320 | tf_op jit(solution)/shard_map/all_to_all | solution.py:409
  30.5 1.2 %collective-permute-start = (bf16[512,512]{1,0:T(8,128)(2,1)S(1)}, bf16[512,512]{1,0:T(8,128)(2,1)S(1)}, u32[]{:S(2)}, u32[]{:S(2)}) collective-permute-start(bf16[512,512]{1,0:T(8,128)(2,1)S(1)} %bitcast.14), channel_id=1, source_target_pairs={{0,64},{64,128},{128,192},{192,0},{1,65},{65,129},{129,193},{193,1... | collective-permute-start | bytes 1572872 | tf_op jit(solution)/shard_map/ppermute | solution.py:424
  31.7 2.5 %collective-permute-start.1 = (bf16[512,512]{1,0:T(8,128)(2,1)S(1)}, bf16[512,512]{1,0:T(8,128)(2,1)S(1)}, u32[]{:S(2)}, u32[]{:S(2)}) collective-permute-start(bf16[512,512]{1,0:T(8,128)(2,1)S(1)} %bitcast.15), channel_id=1, source_target_pairs={{0,128},{64,192},{128,0},{192,64},{1,129},{65,193},{129,1},{193,65... | collective-permute-start | bytes 1572872 | tf_op jit(solution)/shard_map/ppermute | solution.py:424
  34.2 1.2 %collective-permute-start.2 = (bf16[512,512]{1,0:T(8,128)(2,1)S(1)}, bf16[512,512]{1,0:T(8,128)(2,1)S(1)}, u32[]{:S(2)}, u32[]{:S(2)}) collective-permute-start(bf16[512,512]{1,0:T(8,128)(2,1)S(1)} %bitcast.16), channel_id=1, source_target_pairs={{0,192},{64,0},{128,64},{192,128},{1,193},{65,1},{129,65},{193,129... | collective-permute-start | bytes 1572872 | tf_op jit(solution)/shard_map/ppermute | solution.py:424
  35.3 8.2 %stats.1 = (f32[32,4,512]{2,1,0:T(4,128)}, f32[512,128]{1,0:T(8,128)}, f32[512,128]{1,0:T(8,128)}) custom-call(bf16[512,512]{1,0:T(8,128)(2,1)S(1)} %bitcast.17, bf16[512,512]{1,0:T(8,128)(2,1)S(1)} %bitcast.18, bf16[8192,256]{1,0:T(8,128)(2,1)} %book_ref.7, f32[512,256]{1,0:T(8,128)} %pick.1.rows_hbm), custom_call_target="tpu_custom_call" | custom-call | flops 4294967296 | bytes 4194304 | tf_op jit(solution)/shard_map/stats/pallas_call | solution.py:129
  43.6 5.3 %all-to-all-start.1 = ((f32[32,4,512]{2,1,0:T(4,128)}), f32[32,4,512]{2,1,0:T(4,128)S(1)}, u32[]{:S(2)}, u32[]{:S(2)}) async-start(f32[32,4,512]{2,1,0:T(4,128)} %get-tuple-element.12), calls=%async_computation.1 | async-start | bytes 524288 | tf_op jit(solution)/shard_map/all_to_all | solution.py:421
  48.8 1.1 %constant_dynamic-slice_fusion.book_ref = bf16[1024,256]{1,0:T(8,128)(2,1)S(1)} fusion(bf16[8192,256]{1,0:T(8,128)(2,1)} %book_ref.7, s32[]{:T(128)S(6)} %select_n.3), kind=kLoop, calls=%fused_computation.1 | loop fusion | bytes 1048580 | tf_op jit(solution)/shard_map/dynamic_slice | solution.py:418
  49.9 2.7 %collective-permute-start.3 = (bf16[512,512]{1,0:T(8,128)(2,1)S(1)}, bf16[512,512]{1,0:T(8,128)(2,1)S(1)}, u32[]{:S(2)}, u32[]{:S(2)}) collective-permute-start(bf16[512,512]{1,0:T(8,128)(2,1)S(1)} %bitcast.19), channel_id=1, source_target_pairs={{0,32},{32,0},{1,33},{33,1},{2,34},{34,2},{3,35},{35,3},{4,36},{36... | collective-permute-start | bytes 1572872 | tf_op jit(solution)/shard_map/ppermute | solution.py:437
  52.7 0.1 collective-permute-start.4
  52.8 2.2 %collective-permute-done.1.rest_2_ = bf16[512,512]{1,0:T(8,128)(2,1)S(1)} collective-permute-done((bf16[512,512]{1,0:T(8,128)(2,1)S(1)}, bf16[512,512]{1,0:T(8,128)(2,1)S(1)}, u32[]{:S(2)}, u32[]{:S(2)}) %collective-permute-start.1) | collective-permute-done | bytes 524320 | tf_op jit(solution)/shard_map/ppermute | solution.py:424
  55.0 3.3 %collective-permute-start.5 = (bf16[512,512]{1,0:T(8,128)(2,1)S(1)}, bf16[512,512]{1,0:T(8,128)(2,1)}, u32[]{:S(2)}, u32[]{:S(2)}) collective-permute-start(bf16[512,512]{1,0:T(8,128)(2,1)S(1)} %collective-permute-done.1.rest_2_), channel_id=1, source_target_pairs={{0,32},{32,0},{1,33},{33,1},{2,34},{34,2},{3,35},{35,3},{4,36},{36... | collective-permute-start | bytes 1572872 | tf_op jit(solution)/shard_map/ppermute | solution.py:437
  58.3 7.3 %lat_first.1 = (f32[512,256]{1,0:T(8,128)}, f32[512,256]{1,0:T(8,128)}) custom-call(bf16[512,512]{1,0:T(8,128)(2,1)S(1)} %bitcast.20, bf16[512,512]{1,0:T(8,128)(2,1)S(1)} %bitcast.21, f32[512,128]{1,0:T(8,128)} %get-tuple-element.14.m_ref.m_hbm, f32[512,128]{1,0:T(8,128)} %get-tuple-element.15.mean_ref.mean_hbm, bf16[8192,256]{1,0:T(8,128)(2,1)} %book_ref.7), custom_call_target="tpu_custom_call" | custom-call | flops 4294967296 | bytes 2097152 | tf_op jit(solution)/shard_map/lat_first/pallas_call | solution.py:228
  65.6 0.8 combine.1
  66.3 4.0 %all-to-all-start.2 = ((f32[8,4,512]{2,1,0:T(4,128)}), f32[8,4,512]{2,1,0:T(4,128)S(1)}, u32[]{:S(2)}, u32[]{:S(2)}) async-start(f32[8,4,512]{2,1,0:T(4,128)} %get-tuple-element.13.all_ref), calls=%async_computation.2 | async-start | bytes 131072 | tf_op jit(solution)/shard_map/all_to_all | solution.py:428
  70.4 6.4 %lat_second.1 = bf16[512,256]{1,0:T(8,128)(2,1)} custom-call(bf16[512,512]{1,0:T(8,128)(2,1)S(1)} %bitcast.22, bf16[512,512]{1,0:T(8,128)(2,1)S(1)} %bitcast.23, bf16[8192,256]{1,0:T(8,128)(2,1)} %book_ref.7, f32[8,4,512]{2,1,0:T(4,128)} %get-tuple-element.13.all_ref, f32[512,128]{1,0:T(8,128)} %get-tuple-element.14.m_ref.m_hbm, ...), custom_call_target="tpu_custom_call" | custom-call | flops 3221225472 | bytes 2097152 | tf_op jit(solution)/shard_map/lat_second/pallas_call | solution.py:245
  76.8 5.3 %all-to-all-start.3 = ((bf16[32,16,256]{2,1,0:T(8,128)(2,1)}), bf16[32,16,256]{2,1,0:T(8,128)(2,1)S(1)}, u32[]{:S(2)}, u32[]{:S(2)}) async-start(bf16[32,16,256]{2,1,0:T(8,128)(2,1)} %bitcast.3), calls=%async_computation.3 | async-start | bytes 524288 | tf_op jit(solution)/shard_map/all_to_all | solution.py:431
  82.1 13.4 %book_grad.1 = f32[1024,256]{1,0:T(8,128)} custom-call(s32[9]{0:T(128)S(1)} %stack.39.s_ref, f32[8,4,512]{2,1,0:T(4,128)S(1)} %all-to-all-done.2.rows_ref, bf16[1024,256]{1,0:T(8,128)(2,1)S(1)} %constant_dynamic-slice_fusion.book_ref, bf16[512,512]{1,0:T(8,128)(2,1)S(1)} %bitcast.24, bf16[512,512]{1,0:T(8,128)(2,1)S(1)} %collective-permute-done.rest_1_, ...), custom_call_target="tpu_custom_call" | custom-call | flops 8589934592 | bytes 4194304 | tf_op jit(solution)/shard_map/book_grad/pallas_call | solution.py:353
  95.6 0.6 sum_parts.1
  (12 shorter events, 0.0 us)
Async XLA Ops:
  2.2 28.3 %all-to-all-start = ((bf16[32,16,512]{2,1,0:T(8,128)(2,1)}), bf16[32,16,512]{2,1,0:T(8,128)(2,1)S(1)}, u32[]{:S(2)}, u32[]{:S(2)}) async-start(bf16[32,16,512]{2,1,0:T(8,128)(2,1)} %spread.1), calls=%async_computation | async-start | bytes 1048576 | tf_op jit(solution)/shard_map/all_to_all | solution.py:409
  30.5 22.2 %collective-permute-start = (bf16[512,512]{1,0:T(8,128)(2,1)S(1)}, bf16[512,512]{1,0:T(8,128)(2,1)S(1)}, u32[]{:S(2)}, u32[]{:S(2)}) collective-permute-start(bf16[512,512]{1,0:T(8,128)(2,1)S(1)} %bitcast.14), channel_id=1, source_target_pairs={{0,64},{64,128},{128,192},{192,0},{1,65},{65,129},{129,193},{193,1... | collective-permute-start | bytes 1572872 | tf_op jit(solution)/shard_map/ppermute | solution.py:424
  31.7 23.3 %collective-permute-start.1 = (bf16[512,512]{1,0:T(8,128)(2,1)S(1)}, bf16[512,512]{1,0:T(8,128)(2,1)S(1)}, u32[]{:S(2)}, u32[]{:S(2)}) collective-permute-start(bf16[512,512]{1,0:T(8,128)(2,1)S(1)} %bitcast.15), channel_id=1, source_target_pairs={{0,128},{64,192},{128,0},{192,64},{1,129},{65,193},{129,1},{193,65... | collective-permute-start | bytes 1572872 | tf_op jit(solution)/shard_map/ppermute | solution.py:424
  34.2 24.1 %collective-permute-start.2 = (bf16[512,512]{1,0:T(8,128)(2,1)S(1)}, bf16[512,512]{1,0:T(8,128)(2,1)S(1)}, u32[]{:S(2)}, u32[]{:S(2)}) collective-permute-start(bf16[512,512]{1,0:T(8,128)(2,1)S(1)} %bitcast.16), channel_id=1, source_target_pairs={{0,192},{64,0},{128,64},{192,128},{1,193},{65,1},{129,65},{193,129... | collective-permute-start | bytes 1572872 | tf_op jit(solution)/shard_map/ppermute | solution.py:424
  43.6 22.0 %all-to-all-start.1 = ((f32[32,4,512]{2,1,0:T(4,128)}), f32[32,4,512]{2,1,0:T(4,128)S(1)}, u32[]{:S(2)}, u32[]{:S(2)}) async-start(f32[32,4,512]{2,1,0:T(4,128)} %get-tuple-element.12), calls=%async_computation.1 | async-start | bytes 524288 | tf_op jit(solution)/shard_map/all_to_all | solution.py:421
  49.9 32.2 %collective-permute-start.3 = (bf16[512,512]{1,0:T(8,128)(2,1)S(1)}, bf16[512,512]{1,0:T(8,128)(2,1)S(1)}, u32[]{:S(2)}, u32[]{:S(2)}) collective-permute-start(bf16[512,512]{1,0:T(8,128)(2,1)S(1)} %bitcast.19), channel_id=1, source_target_pairs={{0,32},{32,0},{1,33},{33,1},{2,34},{34,2},{3,35},{35,3},{4,36},{36... | collective-permute-start | bytes 1572872 | tf_op jit(solution)/shard_map/ppermute | solution.py:437
  52.7 29.4 %collective-permute-start.4 = (bf16[512,512]{1,0:T(8,128)(2,1)S(1)}, bf16[512,512]{1,0:T(8,128)(2,1)}, u32[]{:S(2)}, u32[]{:S(2)}) collective-permute-start(bf16[512,512]{1,0:T(8,128)(2,1)S(1)} %collective-permute-done.rest_1_), channel_id=1, source_target_pairs={{0,32},{32,0},{1,33},{33,1},{2,34},{34,2},{3,35},{35,3},{4,36},{36... | collective-permute-start | bytes 1572872 | tf_op jit(solution)/shard_map/ppermute | solution.py:437
  55.0 27.1 %collective-permute-start.5 = (bf16[512,512]{1,0:T(8,128)(2,1)S(1)}, bf16[512,512]{1,0:T(8,128)(2,1)}, u32[]{:S(2)}, u32[]{:S(2)}) collective-permute-start(bf16[512,512]{1,0:T(8,128)(2,1)S(1)} %collective-permute-done.1.rest_2_), channel_id=1, source_target_pairs={{0,32},{32,0},{1,33},{33,1},{2,34},{34,2},{3,35},{35,3},{4,36},{36... | collective-permute-start | bytes 1572872 | tf_op jit(solution)/shard_map/ppermute | solution.py:437
  58.3 23.8 %collective-permute-start.6 = (bf16[512,512]{1,0:T(8,128)(2,1)S(1)}, bf16[512,512]{1,0:T(8,128)(2,1)}, u32[]{:S(2)}, u32[]{:S(2)}) collective-permute-start(bf16[512,512]{1,0:T(8,128)(2,1)S(1)} %collective-permute-done.2.rest_3_), channel_id=1, source_target_pairs={{0,32},{32,0},{1,33},{33,1},{2,34},{34,2},{3,35},{35,3},{4,36},{36... | collective-permute-start | bytes 1572872 | tf_op jit(solution)/shard_map/ppermute | solution.py:437
  58.3 7.3 %copy-start = (s32[512]{0:T(512)S(1)}, s32[512]{0:T(512)}, u32[]{:S(2)}) copy-start(s32[512]{0:T(512)} %param.6) | copy-start | bytes 6148
  66.3 10.5 %all-to-all-start.2 = ((f32[8,4,512]{2,1,0:T(4,128)}), f32[8,4,512]{2,1,0:T(4,128)S(1)}, u32[]{:S(2)}, u32[]{:S(2)}) async-start(f32[8,4,512]{2,1,0:T(4,128)} %get-tuple-element.13.all_ref), calls=%async_computation.2 | async-start | bytes 131072 | tf_op jit(solution)/shard_map/all_to_all | solution.py:428
  76.8 18.7 %all-to-all-start.3 = ((bf16[32,16,256]{2,1,0:T(8,128)(2,1)}), bf16[32,16,256]{2,1,0:T(8,128)(2,1)S(1)}, u32[]{:S(2)}, u32[]{:S(2)}) async-start(bf16[32,16,256]{2,1,0:T(8,128)(2,1)} %bitcast.3), calls=%async_computation.3 | async-start | bytes 524288 | tf_op jit(solution)/shard_map/all_to_all | solution.py:431

commit v4 on v3

--- a/solution.py
+++ b/solution.py
@@ -221,9 +221,9 @@
     ]
 
 
-def lat_first(toks, m_col, mean_col, book, part=1, parts=2, cb=2048, sub=512):
+def lat_first(toks, m_col, mean_col, book, sub=512):
     tokens, (codes, d) = toks.shape[0], book.shape
-    steps = codes // cb * part // parts
+    steps, cb = 2, codes * 5 // 16
     whole = pl.BlockSpec((tokens, d), lambda i: (0, 0))
     return pl.pallas_call(
         functools.partial(first_kernel, sub),
@@ -237,10 +237,9 @@
     )(toks, toks, m_col, mean_col, book)
 
 
-def lat_second(toks, m_col, mean_col, book, a, b, rows, row, part=1, parts=2, cb=2048, sub=512):
+def lat_second(toks, m_col, mean_col, book, a, b, rows, row, sub=512):
     tokens, (codes, d) = toks.shape[0], book.shape
-    first = codes // cb * part // parts
-    steps = codes // cb - first
+    first, steps, cb = 5, 3, codes // 8
     whole = pl.BlockSpec((tokens, d), lambda i: (0, 0))
     return pl.pallas_call(
         functools.partial(second_kernel, steps, sub),
@@ -253,7 +252,7 @@
         ]
         + [pl.BlockSpec(memory_space=pltpu.HBM)] * 5,
         out_specs=whole,
-        out_shape=jax.ShapeDtypeStruct((tokens, d), BF16),
+        out_shape=jax.ShapeDtypeStruct((tokens, d), F32),
         scratch_shapes=[pltpu.VMEM((tokens, d), F32)]
         + [pltpu.VMEM((tokens, 128), F32)] * 4
         + [pltpu.VMEM((tokens, d), F32)] * 3

time: 96.9 us -> 105 us (1.084)
  waiting for transfers between devices: 11.9 us -> 17.8 us
  starting transfers between devices: 37.5 us -> 38.6 us
    all_to_all x1, waiting for transfers between devices: 9.68 us -> 15.6 us  [per_device(): toks = lax.all_to_all(spread(*in_hbm(latents, out_grad), peers), ZY, 0, 0)]
    ppermute x4, starting transfers between devices: 6.14 us -> 3.65 us  [per_device(): other.append(lax.ppermute(piece, 'core', swap))]
    ppermute x3, waiting for transfers between devices: 2.22 us -> 0.01 us  [per_device(): same.append(lax.ppermute(toks, 'x', [(i, (i + k) % nx) for i in range(nx)]))]
    all_to_all x1, starting transfers between devices: 5.26 us -> 7.43 us  [per_device(): moved = lax.all_to_all(part.reshape(peers, own_count, d), ZY, 0, 0)]
    all_to_all x1, waiting for transfers between devices: 0.01 us -> 2.14 us  [per_device(): moved = lax.all_to_all(part.reshape(peers, own_count, d), ZY, 0, 0)]
    all_to_all x1, starting transfers between devices: 4.04 us -> 5.43 us  [per_device(): everyone = lax.all_to_all(row, XC, 0, 0)]
    pallas_call x1, Pallas kernels: 7.26 us -> 8.44 us  [lat_first(): pl.pallas_call(functools.partial(first_kernel, sub), grid=(steps,), in_sp...]
  transfers between devices with their start and end apart: 11 -> 11, of which waited for: 2 -> 2; matrix products, arithmetic and copies ran while one was open for 2% -> 2% of each run, Pallas kernels for 43% -> 41%
where the time goes in v4:
time: 105 us; the launch traced here: 103 us
  Pallas kernels  44.4 us (42%)
  starting transfers between devices  38.6 us (37%)
  waiting for transfers between devices  17.8 us (17%)
  local copies, waits for them, and re-layouts  1.29 us (1%)
    all_to_all x1, waiting for transfers between devices, per_device(): toks = lax.all_to_all(spread(*in_hbm(latents, out_grad), peers), ZY, 0, 0)  15.6 us
    pallas_call x1, Pallas kernels, book_grad(): pl.pallas_call(functools.partial(book_kernel, sub, batch), grid_spec=grid...  13.2 us
    all_to_all x1, starting transfers between devices, per_device(): toks = lax.all_to_all(spread(*in_hbm(latents, out_grad), peers), ZY, 0, 0)  12 us
    pallas_call x1, Pallas kernels, lat_first(): pl.pallas_call(functools.partial(first_kernel, sub), grid=(steps,), in_sp...  8.44 us
    pallas_call x1, Pallas kernels, local_stats(): pl.pallas_call(functools.partial(stats_kernel, steps, sub), grid=(steps,)...  8.24 us
    all_to_all x1, starting transfers between devices, per_device(): moved = lax.all_to_all(part.reshape(peers, own_count, d), ZY, 0, 0)  7.43 us
    pallas_call x1, Pallas kernels, lat_second(): pl.pallas_call(functools.partial(second_kernel, steps, sub), grid=(steps,...  5.87 us
    pallas_call x1, Pallas kernels, pick_rows(): pl.pallas_call(functools.partial(pick_kernel, cb), grid=(codes // cb,), i...  5.65 us
  transfers between devices with their start and end apart: 11, of which 2 were waited for; matrix products, arithmetic and copies ran while one was open for 2% of the time, Pallas kernels for 41%

profile of v4, /device:TPU:1, one launch (start us, length us, event | category | flops | bytes accessed | tf_op | source)
XLA Modules:
  0.0 103.5 jit_solution(12154009066894548693)
XLA Ops:
  0.6 1.6 %spread.1 = bf16[32,16,512]{2,1,0:T(8,128)(2,1)} custom-call(bf16[16,256]{1,0:T(8,128)(2,1)} %lat_ref.1, bf16[16,256]{1,0:T(8,128)(2,1)} %grad_ref.1), custom_call_target="tpu_custom_call" | custom-call | tf_op jit(solution)/shard_map/spread/pallas_call | solution.py:371
  2.2 12.0 %all-to-all-start = ((bf16[32,16,512]{2,1,0:T(8,128)(2,1)}), bf16[32,16,512]{2,1,0:T(8,128)(2,1)S(1)}, u32[]{:S(2)}, u32[]{:S(2)}) async-start(bf16[32,16,512]{2,1,0:T(8,128)(2,1)} %spread.1), calls=%async_computation | async-start | bytes 1048576 | tf_op jit(solution)/shard_map/all_to_all | solution.py:408
  14.2 0.7 broadcast_subtract_fusion
  14.9 15.6 %all-to-all-done = bf16[32,16,512]{2,1,0:T(8,128)(2,1)S(1)} async-done(((bf16[32,16,512]{2,1,0:T(8,128)(2,1)}), bf16[32,16,512]{2,1,0:T(8,128)(2,1)S(1)}, u32[]{:S(2)}, u32[]{:S(2)}) %all-to-all-start) | async-done | bytes 524320 | tf_op jit(solution)/shard_map/all_to_all | solution.py:408
  30.5 1.2 %collective-permute-start = (bf16[512,512]{1,0:T(8,128)(2,1)S(1)}, bf16[512,512]{1,0:T(8,128)(2,1)S(1)}, u32[]{:S(2)}, u32[]{:S(2)}) collective-permute-start(bf16[512,512]{1,0:T(8,128)(2,1)S(1)} %bitcast.14), channel_id=1, source_target_pairs={{0,64},{64,128},{128,192},{192,0},{1,65},{65,129},{129,193},{193,1... | collective-permute-start | bytes 1572872 | tf_op jit(solution)/shard_map/ppermute | solution.py:423
  31.7 2.5 %collective-permute-start.1 = (bf16[512,512]{1,0:T(8,128)(2,1)S(1)}, bf16[512,512]{1,0:T(8,128)(2,1)S(1)}, u32[]{:S(2)}, u32[]{:S(2)}) collective-permute-start(bf16[512,512]{1,0:T(8,128)(2,1)S(1)} %bitcast.15), channel_id=1, source_target_pairs={{0,128},{64,192},{128,0},{192,64},{1,129},{65,193},{129,1},{193,65... | collective-permute-start | bytes 1572872 | tf_op jit(solution)/shard_map/ppermute | solution.py:423
  34.2 1.2 %collective-permute-start.2 = (bf16[512,512]{1,0:T(8,128)(2,1)S(1)}, bf16[512,512]{1,0:T(8,128)(2,1)S(1)}, u32[]{:S(2)}, u32[]{:S(2)}) collective-permute-start(bf16[512,512]{1,0:T(8,128)(2,1)S(1)} %bitcast.16), channel_id=1, source_target_pairs={{0,192},{64,0},{128,64},{192,128},{1,193},{65,1},{129,65},{193,129... | collective-permute-start | bytes 1572872 | tf_op jit(solution)/shard_map/ppermute | solution.py:423
  35.3 0.1 broadcast_in_dim.4.tgt_ref
  35.5 5.6 %pick.1.rows_hbm = f32[512,256]{1,0:T(8,128)} custom-call(s32[512,128]{1,0:T(8,128)S(1)} %broadcast_in_dim.4.tgt_ref, bf16[8192,256]{1,0:T(8,128)(2,1)} %book_ref.7), custom_call_target="tpu_custom_call" | custom-call | flops 2147483648 | bytes 4194304 | tf_op jit(solution)/shard_map/pick/pallas_call | solution.py:49
  41.1 8.2 %stats.1 = (f32[32,4,512]{2,1,0:T(4,128)}, f32[512,128]{1,0:T(8,128)}, f32[512,128]{1,0:T(8,128)}) custom-call(bf16[512,512]{1,0:T(8,128)(2,1)S(1)} %bitcast.17, bf16[512,512]{1,0:T(8,128)(2,1)S(1)} %bitcast.18, bf16[8192,256]{1,0:T(8,128)(2,1)} %book_ref.7, f32[512,256]{1,0:T(8,128)} %pick.1.rows_hbm), custom_call_target="tpu_custom_call" | custom-call | flops 4294967296 | bytes 4194304 | tf_op jit(solution)/shard_map/stats/pallas_call | solution.py:129
  49.4 5.3 %all-to-all-start.1 = ((f32[32,4,512]{2,1,0:T(4,128)}), f32[32,4,512]{2,1,0:T(4,128)S(1)}, u32[]{:S(2)}, u32[]{:S(2)}) async-start(f32[32,4,512]{2,1,0:T(4,128)} %get-tuple-element.12), calls=%async_computation.1 | async-start | bytes 524288 | tf_op jit(solution)/shard_map/all_to_all | solution.py:420
  54.6 2.7 %collective-permute-start.3 = (bf16[512,512]{1,0:T(8,128)(2,1)S(1)}, bf16[512,512]{1,0:T(8,128)(2,1)S(1)}, u32[]{:S(2)}, u32[]{:S(2)}) collective-permute-start(bf16[512,512]{1,0:T(8,128)(2,1)S(1)} %bitcast.19), channel_id=1, source_target_pairs={{0,32},{32,0},{1,33},{33,1},{2,34},{34,2},{3,35},{35,3},{4,36},{36... | collective-permute-start | bytes 1572872 | tf_op jit(solution)/shard_map/ppermute | solution.py:436
  57.4 0.1 collective-permute-start.4
  57.5 0.8 collective-permute-start.5
  58.3 8.4 %lat_first.1 = (f32[512,256]{1,0:T(8,128)}, f32[512,256]{1,0:T(8,128)}) custom-call(bf16[512,512]{1,0:T(8,128)(2,1)S(1)} %bitcast.20, bf16[512,512]{1,0:T(8,128)(2,1)S(1)} %bitcast.21, f32[512,128]{1,0:T(8,128)} %get-tuple-element.14.m_ref.m_hbm, f32[512,128]{1,0:T(8,128)} %get-tuple-element.15.mean_ref.mean_hbm, bf16[8192,256]{1,0:T(8,128)(2,1)} %book_ref.7), custom_call_target="tpu_custom_call" | custom-call | flops 5368709120 | bytes 2621440 | tf_op jit(solution)/shard_map/lat_first/pallas_call | solution.py:228
  66.7 0.8 combine.1
  67.5 5.4 %all-to-all-start.2 = ((f32[8,4,512]{2,1,0:T(4,128)}), f32[8,4,512]{2,1,0:T(4,128)S(1)}, u32[]{:S(2)}, u32[]{:S(2)}) async-start(f32[8,4,512]{2,1,0:T(4,128)} %get-tuple-element.13.all_ref), calls=%async_computation.2 | async-start | bytes 131072 | tf_op jit(solution)/shard_map/all_to_all | solution.py:427
  72.9 5.9 %lat_second.1 = f32[512,256]{1,0:T(8,128)} custom-call(bf16[512,512]{1,0:T(8,128)(2,1)S(1)} %bitcast.22, bf16[512,512]{1,0:T(8,128)(2,1)S(1)} %bitcast.23, bf16[8192,256]{1,0:T(8,128)(2,1)} %book_ref.7, f32[8,4,512]{2,1,0:T(4,128)} %get-tuple-element.13.all_ref, f32[512,128]{1,0:T(8,128)} %get-tuple-element.14.m_ref.m_hbm, ...), custom_call_target="tpu_custom_call" | custom-call | flops 2415919104 | bytes 1572864 | tf_op jit(solution)/shard_map/lat_second/pallas_call | solution.py:244
  78.8 7.4 %all-to-all-start.3 = ((f32[32,16,256]{2,1,0:T(8,128)}), f32[32,16,256]{2,1,0:T(8,128)S(1)}, u32[]{:S(2)}, u32[]{:S(2)}) async-start(f32[32,16,256]{2,1,0:T(8,128)} %bitcast.3), calls=%async_computation.3 | async-start | bytes 1048576 | tf_op jit(solution)/shard_map/all_to_all | solution.py:430
  86.3 0.1 stack.39.s_ref
  86.4 1.1 %constant_dynamic-slice_fusion.book_ref = bf16[1024,256]{1,0:T(8,128)(2,1)S(1)} fusion(bf16[8192,256]{1,0:T(8,128)(2,1)} %book_ref.7, s32[]{:T(128)S(6)} %select_n.3), kind=kLoop, calls=%fused_computation.1 | loop fusion | bytes 1048580 | tf_op jit(solution)/shard_map/dynamic_slice | solution.py:417
  87.5 13.2 %book_grad.1 = f32[1024,256]{1,0:T(8,128)} custom-call(s32[9]{0:T(128)S(1)} %stack.39.s_ref, f32[8,4,512]{2,1,0:T(4,128)S(1)} %all-to-all-done.2.rows_ref, bf16[1024,256]{1,0:T(8,128)(2,1)S(1)} %constant_dynamic-slice_fusion.book_ref, bf16[512,512]{1,0:T(8,128)(2,1)S(1)} %bitcast.24, bf16[512,512]{1,0:T(8,128)(2,1)S(1)} %collective-permute-done.rest_1_, ...), custom_call_target="tpu_custom_call" | custom-call | flops 8589934592 | bytes 4194304 | tf_op jit(solution)/shard_map/book_grad/pallas_call | solution.py:352
  100.7 2.1 %all-to-all-done.3.in_ref = f32[32,16,256]{2,1,0:T(8,128)S(1)} async-done(((f32[32,16,256]{2,1,0:T(8,128)}), f32[32,16,256]{2,1,0:T(8,128)S(1)}, u32[]{:S(2)}, u32[]{:S(2)}) %all-to-all-start.3) | async-done | bytes 524320 | tf_op jit(solution)/shard_map/all_to_all | solution.py:430
  102.8 0.6 sum_parts.1
  (12 shorter events, 0.0 us)
Async XLA Ops:
  2.2 28.3 %all-to-all-start = ((bf16[32,16,512]{2,1,0:T(8,128)(2,1)}), bf16[32,16,512]{2,1,0:T(8,128)(2,1)S(1)}, u32[]{:S(2)}, u32[]{:S(2)}) async-start(bf16[32,16,512]{2,1,0:T(8,128)(2,1)} %spread.1), calls=%async_computation | async-start | bytes 1048576 | tf_op jit(solution)/shard_map/all_to_all | solution.py:408
  30.5 26.9 %collective-permute-start = (bf16[512,512]{1,0:T(8,128)(2,1)S(1)}, bf16[512,512]{1,0:T(8,128)(2,1)S(1)}, u32[]{:S(2)}, u32[]{:S(2)}) collective-permute-start(bf16[512,512]{1,0:T(8,128)(2,1)S(1)} %bitcast.14), channel_id=1, source_target_pairs={{0,64},{64,128},{128,192},{192,0},{1,65},{65,129},{129,193},{193,1... | collective-permute-start | bytes 1572872 | tf_op jit(solution)/shard_map/ppermute | solution.py:423
  31.7 25.8 %collective-permute-start.1 = (bf16[512,512]{1,0:T(8,128)(2,1)S(1)}, bf16[512,512]{1,0:T(8,128)(2,1)S(1)}, u32[]{:S(2)}, u32[]{:S(2)}) collective-permute-start(bf16[512,512]{1,0:T(8,128)(2,1)S(1)} %bitcast.15), channel_id=1, source_target_pairs={{0,128},{64,192},{128,0},{192,64},{1,129},{65,193},{129,1},{193,65... | collective-permute-start | bytes 1572872 | tf_op jit(solution)/shard_map/ppermute | solution.py:423
  34.2 24.1 %collective-permute-start.2 = (bf16[512,512]{1,0:T(8,128)(2,1)S(1)}, bf16[512,512]{1,0:T(8,128)(2,1)S(1)}, u32[]{:S(2)}, u32[]{:S(2)}) collective-permute-start(bf16[512,512]{1,0:T(8,128)(2,1)S(1)} %bitcast.16), channel_id=1, source_target_pairs={{0,192},{64,0},{128,64},{192,128},{1,193},{65,1},{129,65},{193,129... | collective-permute-start | bytes 1572872 | tf_op jit(solution)/shard_map/ppermute | solution.py:423
  49.4 17.4 %all-to-all-start.1 = ((f32[32,4,512]{2,1,0:T(4,128)}), f32[32,4,512]{2,1,0:T(4,128)S(1)}, u32[]{:S(2)}, u32[]{:S(2)}) async-start(f32[32,4,512]{2,1,0:T(4,128)} %get-tuple-element.12), calls=%async_computation.1 | async-start | bytes 524288 | tf_op jit(solution)/shard_map/all_to_all | solution.py:420
  54.6 32.8 %collective-permute-start.3 = (bf16[512,512]{1,0:T(8,128)(2,1)S(1)}, bf16[512,512]{1,0:T(8,128)(2,1)S(1)}, u32[]{:S(2)}, u32[]{:S(2)}) collective-permute-start(bf16[512,512]{1,0:T(8,128)(2,1)S(1)} %bitcast.19), channel_id=1, source_target_pairs={{0,32},{32,0},{1,33},{33,1},{2,34},{34,2},{3,35},{35,3},{4,36},{36... | collective-permute-start | bytes 1572872 | tf_op jit(solution)/shard_map/ppermute | solution.py:436
  57.4 30.1 %collective-permute-start.4 = (bf16[512,512]{1,0:T(8,128)(2,1)S(1)}, bf16[512,512]{1,0:T(8,128)(2,1)}, u32[]{:S(2)}, u32[]{:S(2)}) collective-permute-start(bf16[512,512]{1,0:T(8,128)(2,1)S(1)} %collective-permute-done.rest_1_), channel_id=1, source_target_pairs={{0,32},{32,0},{1,33},{33,1},{2,34},{34,2},{3,35},{35,3},{4,36},{36... | collective-permute-start | bytes 1572872 | tf_op jit(solution)/shard_map/ppermute | solution.py:436
  57.5 30.0 %collective-permute-start.5 = (bf16[512,512]{1,0:T(8,128)(2,1)S(1)}, bf16[512,512]{1,0:T(8,128)(2,1)}, u32[]{:S(2)}, u32[]{:S(2)}) collective-permute-start(bf16[512,512]{1,0:T(8,128)(2,1)S(1)} %collective-permute-done.1.rest_2_), channel_id=1, source_target_pairs={{0,32},{32,0},{1,33},{33,1},{2,34},{34,2},{3,35},{35,3},{4,36},{36... | collective-permute-start | bytes 1572872 | tf_op jit(solution)/shard_map/ppermute | solution.py:436
  58.3 29.2 %collective-permute-start.6 = (bf16[512,512]{1,0:T(8,128)(2,1)S(1)}, bf16[512,512]{1,0:T(8,128)(2,1)}, u32[]{:S(2)}, u32[]{:S(2)}) collective-permute-start(bf16[512,512]{1,0:T(8,128)(2,1)S(1)} %collective-permute-done.2.rest_3_), channel_id=1, source_target_pairs={{0,32},{32,0},{1,33},{33,1},{2,34},{34,2},{3,35},{35,3},{4,36},{36... | collective-permute-start | bytes 1572872 | tf_op jit(solution)/shard_map/ppermute | solution.py:436
  58.3 8.5 %copy-start = (s32[512]{0:T(512)S(1)}, s32[512]{0:T(512)}, u32[]{:S(2)}) copy-start(s32[512]{0:T(512)} %param.6) | copy-start | bytes 6148
  67.5 11.3 %all-to-all-start.2 = ((f32[8,4,512]{2,1,0:T(4,128)}), f32[8,4,512]{2,1,0:T(4,128)S(1)}, u32[]{:S(2)}, u32[]{:S(2)}) async-start(f32[8,4,512]{2,1,0:T(4,128)} %get-tuple-element.13.all_ref), calls=%async_computation.2 | async-start | bytes 131072 | tf_op jit(solution)/shard_map/all_to_all | solution.py:427
  78.8 24.0 %all-to-all-start.3 = ((f32[32,16,256]{2,1,0:T(8,128)}), f32[32,16,256]{2,1,0:T(8,128)S(1)}, u32[]{:S(2)}, u32[]{:S(2)}) async-start(f32[32,16,256]{2,1,0:T(8,128)} %bitcast.3), calls=%async_computation.3 | async-start | bytes 1048576 | tf_op jit(solution)/shard_map/all_to_all | solution.py:430
